TPU v7x, 32 devices: a whole 2x2x4 slice. The times are simulated.
32 devices in a mesh: wide: 16 (over z, y, core), narrow: 2 (over x).
Axes of the slice: x: 2, y: 2, z: 4, core: 2. Of those that a mesh axis runs over, the one named last changes fastest.
Arguments:
- frames: bfloat16 [16384, 1024], P(('wide', 'narrow')), may hold values from -6 to 6
- segment_ids: int32 [16, 1024], P('wide', 'narrow'), may hold values from 0 to 3, never falling along the last dimension, each value on 1 to 512 neighbouring positions
- row_length: int32 [16], P('wide'), may hold values from 512 to 1024
- query_proj: bfloat16 [1024, 1024], P('wide', 'narrow'), may hold values from -0.1875 to 0.1875
- key_proj: bfloat16 [1024, 1024], P('wide', 'narrow'), may hold values from -0.1875 to 0.1875
- value_proj: bfloat16 [1024, 1024], P('wide', 'narrow'), may hold values from -0.1875 to 0.1875
- out_proj: bfloat16 [1024, 1024], P('wide', 'narrow'), may hold values from -0.375 to 0.375
- up_proj: bfloat16 [1024, 4096], P('wide', 'narrow'), may hold values from -0.1875 to 0.1875
- down_proj: bfloat16 [4096, 1024], P('wide', 'narrow'), may hold values from -0.09375 to 0.09375
- query_bias: bfloat16 [1024], P(('wide', 'narrow')), may hold values from -1.5 to 1.5
- value_bias: bfloat16 [1024], P(('wide', 'narrow')), may hold values from -1.5 to 1.5
- out_bias: bfloat16 [1024], P(('wide', 'narrow')), may hold values from -1.5 to 1.5
- up_bias: bfloat16 [4096], P(('wide', 'narrow')), may hold values from -1.5 to 1.5
- down_bias: bfloat16 [1024], P(('wide', 'narrow')), may hold values from -1.5 to 1.5
- attn_gain: bfloat16 [1024], P(('wide', 'narrow')), may hold values from 0.5 to 1.5
- mlp_gain: bfloat16 [1024], P(('wide', 'narrow')), may hold values from 0.5 to 1.5
- out_grad: bfloat16 [16384, 1024], P(('wide', 'narrow')), may hold values from -6 to 6
Outputs:
- block_out: bfloat16 [16384, 1024], P(('wide', 'narrow'))
- frames_grad: bfloat16 [16384, 1024], P(('wide', 'narrow'))
- query_proj_grad: float32 [1024, 1024], P('wide', 'narrow')
- key_proj_grad: float32 [1024, 1024], P('wide', 'narrow')
- value_proj_grad: float32 [1024, 1024], P('wide', 'narrow')
- out_proj_grad: float32 [1024, 1024], P('wide', 'narrow')
- up_proj_grad: float32 [1024, 4096], P('wide', 'narrow')
- down_proj_grad: float32 [4096, 1024], P('wide', 'narrow')
- query_bias_grad: float32 [1024], P(('wide', 'narrow'))
- value_bias_grad: float32 [1024], P(('wide', 'narrow'))
- out_bias_grad: float32 [1024], P(('wide', 'narrow'))
- up_bias_grad: float32 [4096], P(('wide', 'narrow'))
- down_bias_grad: float32 [1024], P(('wide', 'narrow'))
- attn_gain_grad: float32 [1024], P(('wide', 'narrow'))
- mlp_gain_grad: float32 [1024], P(('wide', 'narrow'))
Inputs may be any that keep to these rules, and one draw needn't show every extreme that they name: `segment_ids`: segment numbers never fall along a row, and every one of the 4 numbers appears in each row.
All inputs are finite; a program needn't handle non-finite values.
Results may differ from a plain program's by a relative error of at most 0.018.
Values may be sent and summed in bfloat16 or wider, within the bound.
No kernel may reach another device: no remote copies, remote signals or barrier semaphores. Data moves between devices by JAX's collectives and lax.ppermute only.
A program may use at most 256 MiB of HBM per device.

v0:
```python
import math

import jax
import jax.numpy as jnp
from jax import lax
from jax.sharding import PartitionSpec as P

HD = 64


EPS = 1e-05


def product(left, right):
    return jnp.dot(left, right, preferred_element_type=jnp.float32)


def contract_first(left, right):
    return lax.dot_general(
        left, right, (((0,), (0,)), ((), ())), preferred_element_type=jnp.float32
    )


def contract_last(left, right):
    return lax.dot_general(
        left, right, (((1,), (1,)), ((), ())), preferred_element_type=jnp.float32
    )


def rms_scale(values, gain):
    return values * lax.rsqrt(jnp.mean(values * values, axis=-1, keepdims=True) + EPS) * gain


def gather_params(shards):
    inner = (
        lax.all_gather(shards[0], "narrow", axis=1, tiled=True),
        lax.all_gather(shards[1], "narrow", axis=1, tiled=True),
        lax.all_gather(shards[2], "narrow", axis=1, tiled=True),
        lax.all_gather(shards[3], "narrow", axis=1, tiled=True),
        lax.all_gather(shards[4], "narrow", axis=1, tiled=True),
        lax.all_gather(shards[5], "narrow", axis=1, tiled=True),
        lax.all_gather(shards[6], "narrow", axis=1, tiled=True),
    )
    return (
        lax.all_gather(inner[0], "wide", axis=0, tiled=True),
        lax.all_gather(inner[1], "wide", axis=0, tiled=True),
        lax.all_gather(inner[2], "wide", axis=0, tiled=True),
        lax.all_gather(inner[3], "wide", axis=0, tiled=True),
        lax.all_gather(inner[4], "wide", axis=0, tiled=True),
        lax.all_gather(inner[5], "wide", axis=0, tiled=True),
        lax.all_gather(inner[6], "wide", axis=0, tiled=True),
    )


def gather_again(shards):
    inner = (
        lax.all_gather(shards[0], "narrow", axis=1, tiled=True),
        lax.all_gather(shards[1], "narrow", axis=1, tiled=True),
        lax.all_gather(shards[2], "narrow", axis=1, tiled=True),
        lax.all_gather(shards[3], "narrow", axis=1, tiled=True),
        lax.all_gather(shards[4], "narrow", axis=1, tiled=True),
        lax.all_gather(shards[5], "narrow", axis=1, tiled=True),
        lax.all_gather(shards[6], "narrow", axis=1, tiled=True),
    )
    return (
        lax.all_gather(inner[0], "wide", axis=0, tiled=True),
        lax.all_gather(inner[1], "wide", axis=0, tiled=True),
        lax.all_gather(inner[2], "wide", axis=0, tiled=True),
        lax.all_gather(inner[3], "wide", axis=0, tiled=True),
        lax.all_gather(inner[4], "wide", axis=0, tiled=True),
        lax.all_gather(inner[5], "wide", axis=0, tiled=True),
        lax.all_gather(inner[6], "wide", axis=0, tiled=True),
    )


def unpack_vectors(packed, widths):
    table = packed.reshape(-1, packed.shape[-1])
    pieces = []
    offset = 0
    for width in widths:
        pieces.append(table[:, offset : offset + width].reshape(-1).astype(jnp.float32))
        offset = offset + width
    return pieces


def build_mask(own_segments, row_segments, limit, offset, start, count):
    total = row_segments.shape[0]
    rows = offset + start + lax.broadcasted_iota(jnp.int32, (count, total), 0)
    cols = lax.broadcasted_iota(jnp.int32, (count, total), 1)
    same = own_segments[:, None] == row_segments[None, :]
    return (cols <= rows) & same & ((cols < limit) | (cols == rows))


def attend(query_part, key_part, value_part, allowed):
    scale = 1.0 / math.sqrt(HD)
    q3 = query_part.reshape(query_part.shape[0], -1, HD)
    k3 = key_part.reshape(key_part.shape[0], -1, HD)
    v3 = value_part.reshape(value_part.shape[0], -1, HD)
    scores = jnp.einsum("qhd,khd->hqk", q3, k3, preferred_element_type=jnp.float32) * scale
    masked = jnp.where(allowed[None], scores, -1000000000.0)
    top = jnp.max(masked, axis=-1, keepdims=True)
    expo = jnp.exp(masked - top)
    total = jnp.sum(expo, axis=-1, keepdims=True)
    probs = (expo / total).astype(jnp.bfloat16)
    context = jnp.einsum("hqk,khd->qhd", probs, v3, preferred_element_type=jnp.float32)
    return (context.reshape(query_part.shape[0], -1), top + jnp.log(total))


def attend_back(query_part, key_part, value_part, dctx_part, lse_part, allowed):
    scale = 1.0 / math.sqrt(HD)
    q3 = query_part.reshape(query_part.shape[0], -1, HD)
    k3 = key_part.reshape(key_part.shape[0], -1, HD)
    v3 = value_part.reshape(value_part.shape[0], -1, HD)
    d3 = dctx_part.reshape(dctx_part.shape[0], -1, HD)
    scores = jnp.einsum("qhd,khd->hqk", q3, k3, preferred_element_type=jnp.float32) * scale
    masked = jnp.where(allowed[None], scores, -1000000000.0)
    probs32 = jnp.exp(masked - lse_part)
    dprobs = jnp.einsum("qhd,khd->hqk", d3, v3, preferred_element_type=jnp.float32)
    inner = jnp.sum(probs32 * dprobs, axis=-1, keepdims=True)
    dscores = (probs32 * (dprobs - inner)).astype(jnp.bfloat16)
    dquery = jnp.einsum("hqk,khd->qhd", dscores, k3, preferred_element_type=jnp.float32) * scale
    dkey = jnp.einsum("hqk,qhd->khd", dscores, q3, preferred_element_type=jnp.float32) * scale
    dvalue = jnp.einsum(
        "hqk,qhd->khd", probs32.astype(jnp.bfloat16), d3, preferred_element_type=jnp.float32
    )
    return (
        dquery.reshape(query_part.shape[0], -1),
        dkey.reshape(key_part.shape[0], -1),
        dvalue.reshape(key_part.shape[0], -1),
    )


def body(
    frames,
    segment_ids,
    row_length,
    query_proj,
    key_proj,
    value_proj,
    out_proj,
    up_proj,
    down_proj,
    query_bias,
    value_bias,
    out_bias,
    up_bias,
    down_bias,
    attn_gain,
    mlp_gain,
    out_grad,
):
    vectors = (query_bias, value_bias, out_bias, up_bias, down_bias, attn_gain, mlp_gain)
    widths = [piece.shape[0] for piece in vectors]
    packed = jnp.concatenate(vectors).reshape(1, 1, -1)
    shards = (query_proj, key_proj, value_proj, out_proj, up_proj, down_proj, packed)
    full = gather_params(shards)
    w_query, w_key, w_value, w_out, w_up, w_down = (
        full[0],
        full[1],
        full[2],
        full[3],
        full[4],
        full[5],
    )
    b_query, b_value, b_out, b_up, b_down, g_attn, g_mlp = unpack_vectors(full[6], widths)
    length = frames.shape[0]
    own_segments = segment_ids[0]
    limit = row_length[0]
    offset = lax.axis_index("narrow") * length
    frames32 = frames.astype(jnp.float32)
    act_one = rms_scale(frames32, g_attn).astype(jnp.bfloat16)
    queries = (product(act_one, w_query) + b_query).astype(jnp.bfloat16)
    keys = product(act_one, w_key).astype(jnp.bfloat16)
    values = (product(act_one, w_value) + b_value).astype(jnp.bfloat16)
    row_parts = (
        lax.all_gather(keys, "narrow", axis=0, tiled=True),
        lax.all_gather(values, "narrow", axis=0, tiled=True),
        lax.all_gather(own_segments.astype(jnp.bfloat16), "narrow", axis=0, tiled=True),
    )
    row_keys, row_values = (row_parts[0], row_parts[1])
    row_segments = row_parts[2].astype(jnp.int32)
    total = row_keys.shape[0]
    block = min(length, 512)
    starts = list(range(0, length, block))
    masks = [
        build_mask(own_segments, row_segments, limit, offset, start, block) for start in starts
    ]
    width = queries.shape[1]
    group_width = 4 * HD
    firsts = list(range(0, width, group_width))
    context_cols = []
    lse_store = []
    for first in firsts:
        key_group = row_keys[:, first : first + group_width]
        value_group = row_values[:, first : first + group_width]
        pieces = []
        lse_group = []
        for index, start in enumerate(starts):
            piece, lse_part = attend(
                queries[start : start + block, first : first + group_width],
                key_group,
                value_group,
                masks[index],
            )
            pieces.append(piece)
            lse_group.append(lse_part)
        context_cols.append(pieces[0])
        lse_store.append(lse_group)
    context = jnp.concatenate(context_cols, axis=1).astype(jnp.bfloat16)
    mid = frames32 + product(context, w_out) + b_out
    act_two = rms_scale(mid, g_mlp).astype(jnp.bfloat16)
    pre = product(act_two, w_up) + b_up
    hidden = jax.nn.gelu(pre).astype(jnp.bfloat16)
    block_out = (mid + product(hidden, w_down) + b_down).astype(jnp.bfloat16)
    again = gather_again(shards)
    w_query, w_key, w_value, w_out, w_up, w_down = (
        again[0],
        again[1],
        again[2],
        again[3],
        again[4],
        again[5],
    )
    b_query, b_value, b_out, b_up, b_down, g_attn, g_mlp = unpack_vectors(again[6], widths)
    dout32 = out_grad.astype(jnp.float32)
    down_bias_grad = jnp.sum(dout32, axis=0)
    down_grad = contract_first(hidden, out_grad)
    dhidden = contract_last(out_grad, w_down)
    _, gelu_back = jax.vjp(jax.nn.gelu, pre)
    dpre = gelu_back(dhidden)[0].astype(jnp.bfloat16)
    up_bias_grad = jnp.sum(dpre.astype(jnp.float32), axis=0)
    up_grad = contract_first(act_two, dpre)
    dact_two = contract_last(dpre, w_up)
    _, norm_two_back = jax.vjp(rms_scale, mid, g_mlp)
    dmid_norm, mlp_gain_grad = norm_two_back(dact_two)
    dmid = dout32 + dmid_norm
    dattn = dmid.astype(jnp.bfloat16)
    out_bias_grad = jnp.sum(dattn.astype(jnp.float32), axis=0)
    out_grad_w = contract_first(context, dattn)
    dcontext = contract_last(dattn, w_out).astype(jnp.bfloat16)
    dquery_cols = []
    dkey_cols = []
    dvalue_cols = []
    for group_index, first in enumerate(firsts):
        key_group = row_keys[:, first : first + group_width]
        value_group = row_values[:, first : first + group_width]
        dkey_sum = jnp.zeros((total, group_width), jnp.float32)
        dvalue_sum = jnp.zeros((total, group_width), jnp.float32)
        dquery_parts = []
        for index, start in enumerate(starts):
            dquery, dkey, dvalue = attend_back(
                queries[start : start + block, first : first + group_width],
                key_group,
                value_group,
                dcontext[start : start + block, first : first + group_width],
                lse_store[group_index][index],
                masks[index],
            )
            dquery_parts.append(dquery)
            dkey_sum = dkey
            dvalue_sum = dvalue
        dquery_cols.append(dquery_parts[0])
        dkey_cols.append(dkey_sum)
        dvalue_cols.append(dvalue_sum)
    dqueries = jnp.concatenate(dquery_cols, axis=1).astype(jnp.bfloat16)
    dkey_row = jnp.concatenate(dkey_cols, axis=1)
    dvalue_row = jnp.concatenate(dvalue_cols, axis=1)
    own_parts = (
        lax.psum_scatter(
            dkey_row.astype(jnp.bfloat16), "narrow", scatter_dimension=0, tiled=True
        ).astype(jnp.float32),
        lax.psum_scatter(
            dvalue_row.astype(jnp.bfloat16), "narrow", scatter_dimension=0, tiled=True
        ).astype(jnp.float32),
    )
    dkeys = own_parts[0].astype(jnp.bfloat16)
    dvalues = own_parts[1].astype(jnp.bfloat16)
    query_bias_grad = jnp.sum(dqueries.astype(jnp.float32), axis=0)
    value_bias_grad = jnp.sum(dvalues.astype(jnp.float32), axis=0)
    query_grad = contract_first(act_one, dqueries)
    key_grad = contract_first(act_one, dkeys)
    value_grad = contract_first(act_one, dvalues)
    dact_one = (
        contract_last(dqueries, w_query)
        + contract_last(dkeys, w_key)
        + contract_last(dvalues, w_value)
    )
    _, norm_one_back = jax.vjp(rms_scale, frames32, g_attn)
    dframes_norm, attn_gain_grad = norm_one_back(dact_one)
    frames_grad = (dmid + dframes_norm).astype(jnp.bfloat16)
    n_wide = lax.axis_size("wide")
    n_narrow = lax.axis_size("narrow")
    vector_grads = (
        query_bias_grad,
        value_bias_grad,
        out_bias_grad,
        up_bias_grad,
        down_bias_grad,
        attn_gain_grad,
        mlp_gain_grad,
    )
    columns = [
        grad.reshape(n_wide * n_narrow, width_one) for grad, width_one in zip(vector_grads, widths)
    ]
    vector_table = jnp.concatenate(columns, axis=1).reshape(n_wide, n_narrow, -1)
    section = (
        lax.psum_scatter(
            query_grad.astype(jnp.bfloat16), "narrow", scatter_dimension=1, tiled=True
        ).astype(jnp.float32),
        lax.psum_scatter(
            key_grad.astype(jnp.bfloat16), "narrow", scatter_dimension=1, tiled=True
        ).astype(jnp.float32),
        lax.psum_scatter(
            value_grad.astype(jnp.bfloat16), "narrow", scatter_dimension=1, tiled=True
        ).astype(jnp.float32),
        lax.psum_scatter(
            out_grad_w.astype(jnp.bfloat16), "narrow", scatter_dimension=1, tiled=True
        ).astype(jnp.float32),
        lax.psum_scatter(
            up_grad.astype(jnp.bfloat16), "narrow", scatter_dimension=1, tiled=True
        ).astype(jnp.float32),
        lax.psum_scatter(
            down_grad.astype(jnp.bfloat16), "narrow", scatter_dimension=1, tiled=True
        ).astype(jnp.float32),
        lax.psum_scatter(
            vector_table.astype(jnp.bfloat16), "narrow", scatter_dimension=1, tiled=True
        ).astype(jnp.float32),
    )
    final = (
        lax.psum_scatter(
            section[0].astype(jnp.bfloat16), "wide", scatter_dimension=0, tiled=True
        ).astype(jnp.float32),
        lax.psum_scatter(
            section[1].astype(jnp.bfloat16), "wide", scatter_dimension=0, tiled=True
        ).astype(jnp.float32),
        lax.psum_scatter(
            section[2].astype(jnp.bfloat16), "wide", scatter_dimension=0, tiled=True
        ).astype(jnp.float32),
        lax.psum_scatter(
            section[3].astype(jnp.bfloat16), "wide", scatter_dimension=0, tiled=True
        ).astype(jnp.float32),
        lax.psum_scatter(
            section[4].astype(jnp.bfloat16), "wide", scatter_dimension=0, tiled=True
        ).astype(jnp.float32),
        lax.psum_scatter(
            section[5].astype(jnp.bfloat16), "wide", scatter_dimension=0, tiled=True
        ).astype(jnp.float32),
        lax.psum_scatter(
            section[6].astype(jnp.bfloat16), "wide", scatter_dimension=0, tiled=True
        ).astype(jnp.float32),
    )
    flat = final[6].reshape(-1)
    split_grads = []
    offset_one = 0
    for width_one in widths:
        split_grads.append(flat[offset_one : offset_one + width_one])
        offset_one = offset_one + width_one
    return (
        block_out,
        frames_grad,
        final[0],
        final[1],
        final[2],
        final[3],
        final[4],
        final[5],
        split_grads[0],
        split_grads[1],
        split_grads[2],
        split_grads[3],
        split_grads[4],
        split_grads[5],
        split_grads[6],
    )


def solution(mesh):
    return jax.shard_map(
        body,
        mesh=mesh,
        in_specs=(
            P(("wide", "narrow"), None),
            P("wide", "narrow"),
            P("wide"),
            P("wide", "narrow"),
            P("wide", "narrow"),
            P("wide", "narrow"),
            P("wide", "narrow"),
            P("wide", "narrow"),
            P("wide", "narrow"),
            P(("wide", "narrow")),
            P(("wide", "narrow")),
            P(("wide", "narrow")),
            P(("wide", "narrow")),
            P(("wide", "narrow")),
            P(("wide", "narrow")),
            P(("wide", "narrow")),
            P(("wide", "narrow"), None),
        ),
        out_specs=(
            P(("wide", "narrow"), None),
            P(("wide", "narrow"), None),
            P("wide", "narrow"),
            P("wide", "narrow"),
            P("wide", "narrow"),
            P("wide", "narrow"),
            P("wide", "narrow"),
            P("wide", "narrow"),
            P(("wide", "narrow")),
            P(("wide", "narrow")),
            P(("wide", "narrow")),
            P(("wide", "narrow")),
            P(("wide", "narrow")),
            P(("wide", "narrow")),
            P(("wide", "narrow")),
        ),
        check_vma=False,
    )
```

profile of v0, /device:TPU:0, one launch (start us, length us, event | category | flops | bytes accessed | tf_op | source)
XLA Modules:
  0.0 1287.2 jit_solution(5652474123731391789)
XLA Ops:
  38.4 21.9 %all_gather.66 = bf16[16,2,320]{2,1,0:T(2,128)(2,1)S(1)} all-gather(bf16[1,2,320]{2,1,0:T(2,128)(2,1)S(1)} %reshape.458), channel_id=1, replica_groups=mesh['wide'=16,'narrow'=2] {'wide'}, dimensions={0}, use_global_device_ids=true | all-gather | bytes 21760 | tf_op jit(solution)/shard_map/all_gather | solution.py:51
  67.1 32.3 %all-gather.17.cloned.1.call-done = bf16[1024,1024]{1,0:T(8,128)(2,1)} async-done(((bf16[64,1024]{1,0:T(8,128)(2,1)}), bf16[1024,1024]{1,0:T(8,128)(2,1)}) %all-gather.17.cloned.1.call-update) | async-done | bytes 2097168 | tf_op jit(solution)/shard_map/all_gather | solution.py:46
  130.6 11.3 all-gather.15.cloned.1.call-done
  148.3 27.3 %all-gather.13.cloned.1.call-done = bf16[1024,1024]{1,0:T(8,128)(2,1)} async-done(((bf16[512,1024]{1,0:T(8,128)(2,1)}), bf16[1024,1024]{1,0:T(8,128)(2,1)}) %all-gather.13.cloned.1.call-update) | async-done | bytes 2097168 | tf_op jit(solution)/shard_map/all_gather | solution.py:177
  183.1 27.5 %all-gather.19.cloned.1.call-done = bf16[1024,1024]{1,0:T(8,128)(2,1)} async-done(((bf16[512,1024]{1,0:T(8,128)(2,1)}), bf16[1024,1024]{1,0:T(8,128)(2,1)}) %all-gather.19.cloned.1.call-update) | async-done | bytes 2097168 | tf_op jit(solution)/shard_map/all_gather | solution.py:176
  244.5 9.7 all-gather.21.cloned.1.call-done
  258.8 70.5 %all-gather.23.cloned.1.call-done = bf16[1024,4096]{1,0:T(8,128)(2,1)} async-done(((bf16[64,4096]{1,0:T(8,128)(2,1)}), bf16[1024,4096]{1,0:T(8,128)(2,1)}) %all-gather.23.cloned.1.call-update) | async-done | bytes 8388624 | tf_op jit(solution)/shard_map/all_gather | solution.py:49
  329.4 12.0 fusion.75
  341.4 63.1 %all-gather.25.cloned.1.call-done = bf16[4096,1024]{1,0:T(8,128)(2,1)} async-done(((bf16[256,1024]{1,0:T(8,128)(2,1)}), bf16[4096,1024]{1,0:T(8,128)(2,1)}) %all-gather.25.cloned.1.call-update) | async-done | bytes 8388624 | tf_op jit(solution)/shard_map/all_gather | solution.py:50
  404.5 13.7 %fusion.84 = (bf16[4096]{0:T(1024)(128)(2,1)S(1)}, bf16[512,4096]{1,0:T(8,128)(2,1)S(1)}) fusion(f32[512,4096]{1,0:T(8,128)} %fusion.75, f32[4096]{0:T(1024)S(1)} %fusion.68, bf16[512,1024]{1,0:T(8,128)(2,1)S(1)} %copy-done.52, bf16[4096,1024]{1,0:T(8,128)(2,1)} %all-gather.25.cloned.1.call-done), kind=kOutput, calls=%fused_computation.156 | convolution fusion | flops 4341100544 | bytes 22044672 | tf_op jit(solution)/shard_map/dot_general | solution.py:25
  522.5 10.7 reduce-scatter.16.cloned.1.call-done
  537.7 13.1 %convolution_convert_fusion = bf16[4096,1024]{1,0:T(8,128)(2,1)} fusion(bf16[512,1024]{1,0:T(8,128)(2,1)S(1)} %copy-done.53, f32[512,4096]{1,0:T(8,128)} %fusion.75, f32[4096]{0:T(1024)S(1)} %fusion.68), kind=kOutput, calls=%fused_computation.34 | convolution fusion | flops 4320133120 | bytes 17842176 | tf_op jit(solution)/shard_map/dot_general | solution.py:19
  574.4 27.0 %reduce-scatter.20.cloned.1.call-done = bf16[1024,512]{1,0:T(8,128)(2,1)} async-done(((bf16[1024,1024]{1,0:T(8,128)(2,1)}), bf16[1024,512]{1,0:T(8,128)(2,1)}) %reduce-scatter.20.cloned.1.call-update) | async-done | bytes 1048592 | tf_op jit(solution)/shard_map/reduce_scatter | solution.py:307
  601.5 34.1 %reduce-scatter.28.cloned.1.call-done = bf16[1024,512]{1,0:T(8,128)(2,1)} async-done(((bf16[1024,1024]{1,0:T(8,128)(2,1)}), bf16[1024,512]{1,0:T(8,128)(2,1)}) %reduce-scatter.28.cloned.1.call-update) | async-done | bytes 1048592 | tf_op jit(solution)/shard_map/reduce_scatter | solution.py:313
  635.7 34.0 %reduce-scatter.24.cloned.1.call-done = bf16[1024,512]{1,0:T(8,128)(2,1)} async-done(((bf16[1024,1024]{1,0:T(8,128)(2,1)}), bf16[1024,512]{1,0:T(8,128)(2,1)}) %reduce-scatter.24.cloned.1.call-update) | async-done | bytes 1048592 | tf_op jit(solution)/shard_map/reduce_scatter | solution.py:310
  669.7 101.4 %reduce-scatter.40.cloned.1.call-done = bf16[4096,512]{1,0:T(8,128)(2,1)} async-done(((bf16[4096,1024]{1,0:T(8,128)(2,1)}), bf16[4096,512]{1,0:T(8,128)(2,1)}) %reduce-scatter.40.cloned.1.call-update) | async-done | bytes 4194320 | tf_op jit(solution)/shard_map/reduce_scatter | solution.py:322
  771.2 101.4 %reduce-scatter.36.cloned.1.call-done = bf16[1024,2048]{1,0:T(8,128)(2,1)} async-done(((bf16[1024,4096]{1,0:T(8,128)(2,1)}), bf16[1024,2048]{1,0:T(8,128)(2,1)}) %reduce-scatter.36.cloned.1.call-update) | async-done | bytes 4194320 | tf_op jit(solution)/shard_map/reduce_scatter | solution.py:319
  873.4 12.9 %add_convert_fusion = bf16[512,1024]{1,0:T(8,128)(2,1)} fusion(f32[512,1024]{1,0:T(8,128)} %get-tuple-element.61, bf16[4096,1024]{1,0:T(8,128)(2,1)} %all-gather.25.cloned.1.call-done, f32[1024]{0:T(1024)S(1)} %reshape.457, f32[512,4096]{1,0:T(8,128)} %fusion.75, f32[4096]{0:T(1024)S(1)} %fusion.68), kind=kOutput, calls=%fused_computation.78 | convolution fusion | flops 4317511680 | bytes 19943424 | tf_op jit(solution)/shard_map/dot_general | solution.py:15
  888.6 61.1 %all-reduce.1 = bf16[16,1,320]{2,1,0:T(2,128)(2,1)S(1)} all-reduce(bf16[16,1,320]{2,1,0:T(2,128)(2,1)S(1)} %copy.114), channel_id=18, replica_groups=mesh['wide'=16,'narrow'=2] {'wide'}, use_global_device_ids=true, to_apply=%region_38.39.clone | all-reduce | flops 5120 | bytes 20480
  953.1 53.7 %reduce-scatter.22.cloned.1.call-done = bf16[64,512]{1,0:T(8,128)(2,1)} async-done(((bf16[1024,512]{1,0:T(8,128)(2,1)}), bf16[64,512]{1,0:T(8,128)(2,1)}) %reduce-scatter.22.cloned.1.call-update) | async-done | bytes 65552 | tf_op jit(solution)/shard_map/reduce_scatter | solution.py:330
  1008.3 58.6 %reduce-scatter.30.cloned.1.call-done = bf16[64,512]{1,0:T(8,128)(2,1)} async-done(((bf16[1024,512]{1,0:T(8,128)(2,1)}), bf16[64,512]{1,0:T(8,128)(2,1)}) %reduce-scatter.30.cloned.1.call-update) | async-done | bytes 65552 | tf_op jit(solution)/shard_map/reduce_scatter | solution.py:336
  1068.4 58.8 %reduce-scatter.26.cloned.1.call-done = bf16[64,512]{1,0:T(8,128)(2,1)} async-done(((bf16[1024,512]{1,0:T(8,128)(2,1)}), bf16[64,512]{1,0:T(8,128)(2,1)}) %reduce-scatter.26.cloned.1.call-update) | async-done | bytes 65552 | tf_op jit(solution)/shard_map/reduce_scatter | solution.py:333
  1128.7 74.2 %reduce-scatter.42.cloned.1.call-done = bf16[256,512]{1,0:T(8,128)(2,1)} async-done(((bf16[4096,512]{1,0:T(8,128)(2,1)}), bf16[256,512]{1,0:T(8,128)(2,1)}) %reduce-scatter.42.cloned.1.call-update) | async-done | bytes 262160 | tf_op jit(solution)/shard_map/reduce_scatter | solution.py:345
  1204.8 73.9 %reduce-scatter.38.cloned.1.call-done = bf16[64,2048]{1,0:T(8,128)(2,1)} async-done(((bf16[1024,2048]{1,0:T(8,128)(2,1)}), bf16[64,2048]{1,0:T(8,128)(2,1)}) %reduce-scatter.38.cloned.1.call-update) | async-done | bytes 262160 | tf_op jit(solution)/shard_map/reduce_scatter | solution.py:342
  (336 shorter events, 266.1 us)
Async XLA Ops:
  7.2 55.5 %all-gather.11.cloned.1.call-start = ((), (), s32[]{:S(2)}) async-start(), calls=%async_computation.15 | async-start | bytes 2228224 | tf_op jit(solution)/shard_map/all_gather | solution.py:47
  14.9 84.5 %all-gather.17.cloned.1.call-start = ((), (), s32[]{:S(2)}) async-start(), calls=%async_computation.18 | async-start | bytes 2228224 | tf_op jit(solution)/shard_map/all_gather | solution.py:46
  20.2 121.7 %all-gather.15.cloned.1.call-start = ((), (), s32[]{:S(2)}) async-start(), calls=%async_computation.17 | async-start | bytes 2228224 | tf_op jit(solution)/shard_map/all_gather | solution.py:45
  26.4 149.2 %all-gather.13.cloned.1.call-start = ((), (), s32[]{:S(2)}) async-start(), calls=%async_computation.16 | async-start | bytes 3145728 | tf_op jit(solution)/shard_map/all_gather | solution.py:177
  67.0 143.6 %all-gather.19.cloned.1.call-start = ((), (), s32[]{:S(2)}) async-start(), calls=%async_computation.19 | async-start | bytes 3145728 | tf_op jit(solution)/shard_map/all_gather | solution.py:176
  103.3 150.9 %all-gather.21.cloned.1.call-start = ((), (), s32[]{:S(2)}) async-start(), calls=%async_computation.20 | async-start | bytes 2228224 | tf_op jit(solution)/shard_map/all_gather | solution.py:48
  108.4 221.0 %all-gather.23.cloned.1.call-start = ((), (), s32[]{:S(2)}) async-start(), calls=%async_computation.21 | async-start | bytes 8912896 | tf_op jit(solution)/shard_map/all_gather | solution.py:49
  116.6 287.9 %all-gather.25.cloned.1.call-start = ((), (), s32[]{:S(2)}) async-start(), calls=%async_computation.22 | async-start | bytes 8912896 | tf_op jit(solution)/shard_map/all_gather | solution.py:50
  123.8 394.5 %reduce-scatter.18.cloned.1.call-start = ((), (), s32[]{:S(2)}) async-start(), calls=%async_computation.24 | async-start | bytes 3145728 | tf_op jit(solution)/shard_map/reduce_scatter | solution.py:272
  463.7 69.5 %reduce-scatter.16.cloned.1.call-start = ((), (), s32[]{:S(2)}) async-start(), calls=%async_computation.23 | async-start | bytes 3145728 | tf_op jit(solution)/shard_map/reduce_scatter | solution.py:269
  502.6 71.2 %reduce-scatter.32.cloned.1.call-start = ((), (), s32[]{:S(2)}) async-start(), calls=%async_computation.31 | async-start | bytes 3145728 | tf_op jit(solution)/shard_map/reduce_scatter | solution.py:316
  506.5 95.0 %reduce-scatter.20.cloned.1.call-start = ((), (), s32[]{:S(2)}) async-start(), calls=%async_computation.25 | async-start | bytes 3145728 | tf_op jit(solution)/shard_map/reduce_scatter | solution.py:307
  518.3 117.4 %reduce-scatter.28.cloned.1.call-start = ((), (), s32[]{:S(2)}) async-start(), calls=%async_computation.29 | async-start | bytes 3145728 | tf_op jit(solution)/shard_map/reduce_scatter | solution.py:313
  522.5 147.2 %reduce-scatter.24.cloned.1.call-start = ((), (), s32[]{:S(2)}) async-start(), calls=%async_computation.27 | async-start | bytes 3145728 | tf_op jit(solution)/shard_map/reduce_scatter | solution.py:310
  537.3 233.9 %reduce-scatter.40.cloned.1.call-start = ((), (), s32[]{:S(2)}) async-start(), calls=%async_computation.35 | async-start | bytes 12582912 | tf_op jit(solution)/shard_map/reduce_scatter | solution.py:322
  550.8 321.9 %reduce-scatter.36.cloned.1.call-start = ((), (), s32[]{:S(2)}) async-start(), calls=%async_computation.33 | async-start | bytes 12582912 | tf_op jit(solution)/shard_map/reduce_scatter | solution.py:319
  561.5 326.4 %reduce-scatter.44.cloned.1.call-start = ((), (), s32[]{:S(2)}) async-start(), calls=%async_computation.37 | async-start | bytes 36864 | tf_op jit(solution)/shard_map/reduce_scatter | solution.py:325
  573.8 377.8 %reduce-scatter.34.cloned.1.call-start = ((), (), s32[]{:S(2)}) async-start(), calls=%async_computation.32 | async-start | bytes 1114112 | tf_op jit(solution)/shard_map/reduce_scatter | solution.py:339
  574.4 432.4 %reduce-scatter.22.cloned.1.call-start = ((), (), s32[]{:S(2)}) async-start(), calls=%async_computation.26 | async-start | bytes 1114112 | tf_op jit(solution)/shard_map/reduce_scatter | solution.py:330
  601.5 465.5 %reduce-scatter.30.cloned.1.call-start = ((), (), s32[]{:S(2)}) async-start(), calls=%async_computation.30 | async-start | bytes 1114112 | tf_op jit(solution)/shard_map/reduce_scatter | solution.py:336
  635.6 491.6 %reduce-scatter.26.cloned.1.call-start = ((), (), s32[]{:S(2)}) async-start(), calls=%async_computation.28 | async-start | bytes 1114112 | tf_op jit(solution)/shard_map/reduce_scatter | solution.py:333
  669.7 533.3 %reduce-scatter.42.cloned.1.call-start = ((), (), s32[]{:S(2)}) async-start(), calls=%async_computation.36 | async-start | bytes 4456448 | tf_op jit(solution)/shard_map/reduce_scatter | solution.py:345
  771.2 101.6 %copy-start.69 = (u32[32]{0:T(128)S(1)}, u32[32]{0:T(128)}, u32[]{:S(2)}) copy-start(u32[32]{0:T(128)} %constant.53) | copy-start | bytes 388
  771.2 507.5 %reduce-scatter.38.cloned.1.call-start = ((), (), s32[]{:S(2)}) async-start(), calls=%async_computation.34 | async-start | bytes 4456448 | tf_op jit(solution)/shard_map/reduce_scatter | solution.py:342
  (76 other events, 921.2 us)
Sparse Core Ops, SparseCore 0:
  15.0 41.9 all-gather.10
  59.2 40.2 all-gather.16
  101.6 40.3 all-gather.14
  143.9 31.6 all-gather.12
  177.5 33.0 all-gather.18
  212.7 41.4 all-gather.20
  256.4 72.9 all-gather.22
  331.6 72.8 all-gather.24
  463.8 30.4 reduce-scatter.17
  502.8 30.4 reduce-scatter.15
  535.5 31.8 reduce-scatter.31
  569.5 31.8 reduce-scatter.19
  603.7 31.8 reduce-scatter.27
  637.7 31.8 reduce-scatter.23
  671.8 99.3 reduce-scatter.39
  773.3 99.3 reduce-scatter.35
  875.3 9.9 reduce-scatter.43
  888.8 57.7 reduce-scatter.33
  950.1 56.5 reduce-scatter.21
  1010.3 56.6 reduce-scatter.29
  1070.6 56.6 reduce-scatter.25
  1131.1 71.8 reduce-scatter.41
  1206.8 71.8 reduce-scatter.37
where the time goes:
time: 1290 us
  waiting for transfers between devices  871 us (68%)
  matrix products  182 us (14%)
  blocking collectives  132 us (10%)
  other arithmetic  46.1 us (4%)
  local copies, waits for them, and re-layouts  38 us (3%)
  between operations  16.6 us (1%)
    reduce_scatter x1, waiting for transfers between devices, body(): lax.psum_scatter(up_grad.astype(jnp.bfloat16), 'narrow', scatter_dimensio...  101 us
    reduce_scatter x1, waiting for transfers between devices, body(): lax.psum_scatter(down_grad.astype(jnp.bfloat16), 'narrow', scatter_dimens...  101 us
    reduce_scatter x1, waiting for transfers between devices, body(): lax.psum_scatter(section[5].astype(jnp.bfloat16), 'wide', scatter_dimensi...  74.2 us
    reduce_scatter x1, waiting for transfers between devices, body(): lax.psum_scatter(section[4].astype(jnp.bfloat16), 'wide', scatter_dimensi...  73.9 us
    all_gather x1, waiting for transfers between devices, gather_params(): lax.all_gather(inner[4], 'wide', axis=0, tiled=True)  70.5 us
    unnamed x2, blocking collectives  66 us
    all_gather x1, waiting for transfers between devices, gather_params(): lax.all_gather(inner[5], 'wide', axis=0, tiled=True)  63.1 us
    reduce_scatter x1, waiting for transfers between devices, body(): lax.psum_scatter(section[1].astype(jnp.bfloat16), 'wide', scatter_dimensi...  58.8 us
  transfers between devices with their start and end apart: 23, of which 18 were waited for; matrix products, arithmetic and copies ran while one was open for 15% of the time, Pallas kernels for 0%

commit v1 on v0

--- a/solution.py
+++ b/solution.py
@@ -1,14 +1,739 @@
+import functools
 import math
 
 import jax
 import jax.numpy as jnp
 from jax import lax
+from jax.experimental import pallas as pl
+from jax.experimental.pallas import tpu as pltpu
 from jax.sharding import PartitionSpec as P
 
 HD = 64
 
 
 EPS = 1e-05
+
+F32 = jnp.float32
+BF = jnp.bfloat16
+
+
+def dot(left, right):
+    return jnp.dot(left, right, preferred_element_type=F32)
+
+
+def dot_last(left, right):
+    return lax.dot_general(left, right, (((1,), (1,)), ((), ())), preferred_element_type=F32)
+
+
+def dot_first(left, right):
+    return lax.dot_general(left, right, (((0,), (0,)), ((), ())), preferred_element_type=F32)
+
+
+def ds(start, size):
+    return pl.ds(pl.multiple_of(start, size), size)
+
+
+def place(sc, p, nz, ny):
+    zrel, yrel = p % nz, p // nz
+    return lax.rem(sc[0] + nz - zrel, nz) * ny + lax.rem(sc[1] + ny - yrel, ny)
+
+
+def call(kernel, sc, args, grid, in_specs, out_specs, out_shape, scratch=()):
+    spec = pltpu.PrefetchScalarGridSpec(
+        num_scalar_prefetch=1,
+        grid=grid,
+        in_specs=in_specs,
+        out_specs=out_specs,
+        scratch_shapes=list(scratch),
+    )
+    return pl.pallas_call(
+        kernel,
+        grid_spec=spec,
+        out_shape=out_shape,
+        compiler_params=pltpu.CompilerParams(dimension_semantics=("arbitrary",) * len(grid)),
+    )(sc, *args)
+
+
+def whole(shape):
+    return pl.BlockSpec(shape, lambda i, sc: (0,) * len(shape), pipeline_mode=pl.Buffered(1))
+
+
+def sds(shape, dtype):
+    return jax.ShapeDtypeStruct(shape, dtype)
+
+
+def qkv_kernel(
+    sc, own, oth, gain, qb, vb, wa0, wa1, wb0, wb1, q_o, k_o, v_o, a_o, tmp, *, nz, ny, blk, grp
+):
+    i = pl.program_id(0)
+    half = pl.num_programs(0) // 2
+    mine = i // half == sc[3]
+    f = jnp.where(mine, own[...].astype(F32), oth[...].astype(F32))
+    r = lax.rsqrt(jnp.mean(f * f, axis=1, keepdims=True) + EPS)
+    tmp[...] = (f * r * gain[...]).astype(BF)
+    for p in range(nz * ny):
+        a_o[:, p * blk : (p + 1) * blk] = tmp[:, ds(place(sc, p, nz, ny) * blk, blk)]
+    k = nz * blk
+    for g, (w0, w1) in enumerate(((wa0, wa1), (wb0, wb1))):
+        res = dot(a_o[:, :k], w0[...].reshape(k, 3 * grp))
+        res = res + dot(a_o[:, k:], w1[...].reshape(k, 3 * grp))
+        lo, hi = g * grp, (g + 1) * grp
+        q_o[:, lo:hi] = (res[:, :grp] + qb[:, lo:hi]).astype(BF)
+        k_o[:, lo:hi] = res[:, grp : 2 * grp].astype(BF)
+        v_o[:, lo:hi] = (res[:, 2 * grp :] + vb[:, lo:hi]).astype(BF)
+
+
+def fill_bias(sc, segc, segr, bias, qb):
+    total = bias.shape[0]
+    for start in range(0, total, qb):
+        n = start + qb
+        rows = start + lax.broadcasted_iota(jnp.int32, (qb, n), 0)
+        cols = lax.broadcasted_iota(jnp.int32, (qb, n), 1)
+        ok = (cols <= rows) & (segc[start:n, :] == segr[:, :n])
+        ok = ok & ((cols < sc[4]) | (cols == rows))
+        bias[start:n, :n] = jnp.where(ok, 0.0, -1000000000.0)
+
+
+def attn_kernel(sc, segc, segr, q, k, v, c_o, l_o, bias, *, qb):
+    p = pl.program_id(0)
+    total = q.shape[0]
+
+    @pl.when(p == 0)
+    def _():
+        fill_bias(sc, segc, segr, bias, qb)
+        l_o[...] = jnp.zeros_like(l_o)
+
+    lane = lax.broadcasted_iota(jnp.int32, (qb, 128), 1)
+    for start in range(0, total, qb):
+        n = start + qb
+        outs = []
+        lse = l_o[start:n, :]
+        for h in range(2):
+            lo, hi = h * HD, (h + 1) * HD
+            qh = q[start:n, lo:hi] * jnp.asarray(1.0 / math.sqrt(HD), BF)
+            s = dot_last(qh, k[:n, lo:hi]) + bias[start:n, :n]
+            top = jnp.max(s, axis=1, keepdims=True)
+            e = jnp.exp(s - top)
+            t = jnp.sum(e, axis=1, keepdims=True)
+            pr = (e * (1.0 / t)).astype(BF)
+            outs.append(dot(pr, v[:n, lo:hi]))
+            lse = jnp.where(lane == 2 * p + h, top + jnp.log(t), lse)
+        l_o[start:n, :] = lse
+        c_o[start:n, :] = jnp.concatenate(outs, axis=1).astype(BF)
+
+
+def attn_back_kernel(sc, segc, segr, q, k, v, d, l, dq_o, dk_o, dv_o, bias, dks, dvs, *, qb):
+    p = pl.program_id(0)
+    total = q.shape[0]
+
+    @pl.when(p == 0)
+    def _():
+        fill_bias(sc, segc, segr, bias, qb)
+
+    lane = lax.broadcasted_iota(jnp.int32, (qb, 128), 1)
+    scale = jnp.asarray(1.0 / math.sqrt(HD), BF)
+    for start in range(total - qb, -1, -qb):
+        n = start + qb
+        dqs, dkk, dvv = [], [], []
+        for h in range(2):
+            lo, hi = h * HD, (h + 1) * HD
+            qh = q[start:n, lo:hi] * scale
+            kh, vh, dh = k[:n, lo:hi], v[:n, lo:hi], d[start:n, lo:hi]
+            lse = jnp.sum(jnp.where(lane == 2 * p + h, l[start:n, :], 0.0), axis=1, keepdims=True)
+            pr = jnp.exp(dot_last(qh, kh) + bias[start:n, :n] - lse)
+            dp = dot_last(dh, vh)
+            inner = jnp.sum(pr * dp, axis=1, keepdims=True)
+            dsc = (pr * (dp - inner)).astype(BF)
+            dqs.append(dot(dsc, kh) * (1.0 / math.sqrt(HD)))
+            dkk.append(dot_first(dsc, qh))
+            dvv.append(dot_first(pr.astype(BF), dh))
+        dq_o[start:n, :] = jnp.concatenate(dqs, axis=1).astype(BF)
+        dkk, dvv = jnp.concatenate(dkk, axis=1), jnp.concatenate(dvv, axis=1)
+        if n == total:
+            dks[...] = dkk
+            dvs[...] = dvv
+        else:
+            dks[:n, :] += dkk
+            dvs[:n, :] += dvv
+    dk_o[...] = dks[...].astype(BF)
+    dv_o[...] = dvs[...].astype(BF)
+
+
+def out_weight(wa, wb, xrel, crel, yrel):
+    block = wa[yrel][:, xrel] if crel == 0 else wb[yrel, :, xrel]
+    return block.reshape(block.shape[0] * block.shape[1], block.shape[2])
+
+
+def out_kernel(
+    sc, cown, coth, fr, ob, gain, wa0, wa1, wb, cr_o, mid_o, a_o, cs, ms, *, nz, ny, nx, blk, wc
+):
+    hw = cown.shape[1]
+    x, c = sc[3], sc[2]
+    cs[:, ds(x * hw, hw)] = cown[...]
+    cs[:, ds((1 - x) * hw, hw)] = coth[...]
+    for p in range(nz * ny):
+        cr_o[:, p * blk : (p + 1) * blk] = cs[:, ds(place(sc, p, nz, ny) * blk, blk)]
+    k = nz * blk
+    for xrel in range(nx):
+        for crel in range(2):
+            acc = dot(cr_o[:, :k], out_weight((wa0, wa1), wb, xrel, crel, 0))
+            acc = acc + dot(cr_o[:, k:], out_weight((wa0, wa1), wb, xrel, crel, 1))
+            base = lax.rem(x + xrel, nx) * 2 + lax.rem(c + crel, 2)
+            ms[:, ds(base * wc, wc)] = acc
+    mid = fr[...].astype(F32) + ms[...] + ob[...]
+    mid_o[...] = mid
+    r = lax.rsqrt(jnp.mean(mid * mid, axis=1, keepdims=True) + EPS)
+    cs[...] = (mid * r * gain[...]).astype(BF)
+    for p in range(nz * ny):
+        a_o[:, p * blk : (p + 1) * blk] = cs[:, ds(place(sc, p, nz, ny) * blk, blk)]
+
+
+def mlp_kernel(
+    sc, a0, a1, d0, d1, ub, up0, up1, dn0, dn1,
+    bo_o, bs_o, da_o, ds_o, uo_o, us_o, do_o, dos_o, ug_o,
+    act, act_t, dr, bacc, dacc,
+):
+    t = pl.program_id(0)
+    m = a0.shape[0]
+    hw = dn0.shape[3]
+    x = sc[3]
+
+    @pl.when(t == 0)
+    def _():
+        for row, (a, d) in enumerate(((a0, d0), (a1, d1))):
+            act[row * m : (row + 1) * m, :] = a[...]
+            act_t[:, row * m : (row + 1) * m] = a[...].T
+            dr[row * m : (row + 1) * m, :hw] = d[:, ds(x * hw, hw)]
+            dr[row * m : (row + 1) * m, hw:] = d[:, ds((1 - x) * hw, hw)]
+        bacc[...] = jnp.zeros_like(bacc)
+        dacc[...] = jnp.zeros_like(dacc)
+
+    nz, ff = up0.shape[0], up0.shape[3]
+    k = nz * up0.shape[2]
+    u0 = up0[...].reshape(k, ff)
+    u1 = up1[...].reshape(k, ff)
+    w0 = dn0[...].reshape(ff, hw)
+    w1 = dn1[...].reshape(ff, hw)
+    pre = dot(act[:, :k], u0) + dot(act[:, k:], u1) + ub[...].reshape(1, ff)
+    dh = dot_last(dr[:, :hw], w0) + dot_last(dr[:, hw:], w1)
+    sq = pre * pre
+    th = jnp.tanh(pre * (0.7978845608 + (0.7978845608 * 0.044715) * sq))
+    hp = 0.5 * (1.0 + th)
+    hid = (pre * hp).astype(BF)
+    slope = hp + (0.5 * pre) * (1.0 - th * th) * (
+        0.7978845608 + (3.0 * 0.7978845608 * 0.044715) * sq
+    )
+    dpre = (dh * slope).astype(BF)
+    bacc[:, :hw] += dot(hid, w0)
+    bacc[:, hw:] += dot(hid, w1)
+    dacc[:, :k] += dot_last(dpre, u0)
+    dacc[:, k:] += dot_last(dpre, u1)
+    uo_o[...] = dot(act_t[:k, :], dpre).astype(BF).reshape(1, k, ff)
+    us_o[...] = dot(act_t[k:, :], dpre).astype(BF).reshape(1, k, ff)
+    hid_t = hid.T
+    do_o[...] = dot(hid_t, dr[:, :hw]).astype(BF).reshape(1, ff, hw)
+    dos_o[...] = dot(hid_t, dr[:, hw:]).astype(BF).reshape(1, ff, hw)
+    ug_o[...] = jnp.sum(dpre.astype(F32), axis=0, keepdims=True).reshape(1, 1, ff)
+
+    @pl.when(t == pl.num_programs(0) - 1)
+    def _():
+        bo_o[...] = bacc[:m, :]
+        bs_o[...] = bacc[m:, :].astype(BF)
+        da_o[...] = dacc[:m, :]
+        ds_o[...] = dacc[m:, :].astype(BF)
+
+
+def mid_kernel(
+    sc, da, dr, bo, br, mid, do, gain, db, cr, wa0, wa1, wb,
+    blk_o, dmid_o, dco_o, dcs_o, wo_o, ws_o, vec_o,
+    tmp, dat, dcx, acc_o, acc_s, *, nz, ny, nx, blk, wc,
+):
+    i = pl.program_id(0)
+    x, c = sc[3], sc[2]
+    hw = bo.shape[1] // nx
+
+    @pl.when(i == 0)
+    def _():
+        vec_o[...] = jnp.zeros_like(vec_o)
+        acc_o[...] = jnp.zeros_like(acc_o)
+        acc_s[...] = jnp.zeros_like(acc_s)
+
+    mv = mid[...]
+    for xrel in range(nx):
+        part = bo[:, xrel * hw : (xrel + 1) * hw] + br[:, xrel * hw : (xrel + 1) * hw].astype(F32)
+        tmp[:, ds(lax.rem(x + xrel, nx) * hw, hw)] = part
+    blk_o[...] = (mv + tmp[...] + db[...]).astype(BF)
+    for p in range(nz * ny):
+        part = da[:, p * blk : (p + 1) * blk] + dr[:, p * blk : (p + 1) * blk].astype(F32)
+        tmp[:, ds(place(sc, p, nz, ny) * blk, blk)] = part
+    dact = tmp[...]
+    r = lax.rsqrt(jnp.mean(mv * mv, axis=1, keepdims=True) + EPS)
+    n = mv * r
+    dn = dact * gain[...]
+    dout = do[...].astype(F32)
+    dmid = dout + r * (dn - n * jnp.mean(dn * n, axis=1, keepdims=True))
+    dmid_o[...] = dmid
+    dattn = dmid.astype(BF)
+    dat[...] = dattn
+    vec_o[0:1, :] += jnp.sum(dact * n, axis=0, keepdims=True)
+    vec_o[1:2, :] += jnp.sum(dattn.astype(F32), axis=0, keepdims=True)
+    vec_o[2:3, :] += jnp.sum(dout, axis=0, keepdims=True)
+    k = nz * blk
+    sums = [None, None]
+    crt = cr[...].T
+    for xrel in range(nx):
+        for crel in range(2):
+            base = lax.rem(x + xrel, nx) * 2 + lax.rem(c + crel, 2)
+            piece = dat[:, ds(base * wc, wc)]
+            for yrel in range(2):
+                got = dot_last(piece, out_weight((wa0, wa1), wb, xrel, crel, yrel))
+                sums[yrel] = got if sums[yrel] is None else sums[yrel] + got
+            acc = acc_o if crel == 0 else acc_s
+            acc[:, xrel * wc : (xrel + 1) * wc] += dot(crt, piece)
+    for p in range(nz * ny):
+        part = sums[p // nz][:, (p % nz) * blk : (p % nz + 1) * blk]
+        dcx[:, ds(place(sc, p, nz, ny) * blk, blk)] = part.astype(BF)
+    heads = dco_o.shape[1]
+    dco_o[...] = dcx[:, ds(x * heads, heads)]
+    dcs_o[...] = dcx[:, ds((1 - x) * heads, heads)]
+
+    @pl.when(i == pl.num_programs(0) - 1)
+    def _():
+        wo_o[...] = acc_o[...].astype(BF)
+        ws_o[...] = acc_s[...].astype(BF)
+
+
+def dact_kernel(
+    sc, dq, dk, dv, own, oth, gain, ar, wa0, wa1, wb0, wb1,
+    da_o, ds_o, wo_o, ws_o, vec_o, tmp, acc, *, nz, ny, blk, grp,
+):
+    i = pl.program_id(0)
+    half = pl.num_programs(0) // 2
+
+    @pl.when(i == 0)
+    def _():
+        vec_o[...] = jnp.zeros_like(vec_o)
+        acc[...] = jnp.zeros_like(acc)
+
+    mine = i >= half
+    f = jnp.where(mine, own[...].astype(F32), oth[...].astype(F32))
+    r = lax.rsqrt(jnp.mean(f * f, axis=1, keepdims=True) + EPS)
+    k = nz * blk
+    sums = [None, None]
+    art = ar[...].T
+    for g, pair in enumerate(((wa0, wa1), (wb0, wb1))):
+        lo, hi = g * grp, (g + 1) * grp
+        cat = jnp.concatenate([dq[:, lo:hi], dk[:, lo:hi], dv[:, lo:hi]], axis=1)
+        for yrel in range(2):
+            got = dot_last(cat, pair[yrel][...].reshape(k, 3 * grp))
+            sums[yrel] = got if sums[yrel] is None else sums[yrel] + got
+        acc[:, g * 3 * grp : (g + 1) * 3 * grp] += dot(art, cat)
+    for p in range(nz * ny):
+        part = sums[p // nz][:, (p % nz) * blk : (p % nz + 1) * blk]
+        tmp[:, ds(place(sc, p, nz, ny) * blk, blk)] = part
+    dact = tmp[...]
+    vec_o[0:1, :] += jnp.sum(dact * (f * r), axis=0, keepdims=True)
+    w = 2 * grp
+    vec_o[1:2, :w] += jnp.sum(dq[...].astype(F32), axis=0, keepdims=True)
+    vec_o[2:3, :w] += jnp.sum(dv[...].astype(F32), axis=0, keepdims=True)
+
+    @pl.when(mine)
+    def _():
+        da_o[...] = dact
+
+    @pl.when(i < half)
+    def _():
+        ds_o[...] = dact.astype(BF)
+
+    @pl.when(i == pl.num_programs(0) - 1)
+    def _():
+        wo_o[...] = acc[:, : 3 * grp].astype(BF)
+        ws_o[...] = acc[:, 3 * grp :].astype(BF)
+
+
+def last_kernel(sc, da, dr, dmid, fr, gain, o):
+    f = fr[...].astype(F32)
+    r = lax.rsqrt(jnp.mean(f * f, axis=1, keepdims=True) + EPS)
+    n = f * r
+    dn = (da[...] + dr[...].astype(F32)) * gain[...]
+    o[...] = (dmid[...] + r * (dn - n * jnp.mean(dn * n, axis=1, keepdims=True))).astype(BF)
+
+
+def add_low(*parts):
+    total = parts[0].astype(F32)
+    for part in parts[1:]:
+        total = total + part.astype(F32)
+    return total
+
+
+def fast_body(nz, ny, nx, *args):
+    (
+        frames, segment_ids, row_length, query_proj, key_proj, value_proj, out_proj, up_proj,
+        down_proj, query_bias, value_bias, out_bias, up_bias, down_bias, attn_gain, mlp_gain,
+        out_grad,
+    ) = args
+    nw = nz * ny * 2
+    nb = nz * ny
+    w = lax.axis_index("wide")
+    x = lax.axis_index("narrow")
+    c = lax.rem(w, 2)
+    y = lax.rem(w // 2, ny)
+    z = w // (2 * ny)
+    m, d = frames.shape
+    rows = m * nx
+    blk = d // nb
+    grp = query_proj.shape[1] // 2
+    wr = query_proj.shape[0]
+    ffb = down_proj.shape[0]
+    ffx = up_proj.shape[1] // 2
+    nj = ffx // ffb
+    wc = grp
+    hw = d // nx
+
+    def send_w(a, dz=0, dy=0, dc=0):
+        perm = []
+        for i in range(nw):
+            zi, yi, ci = i // (2 * ny), (i // 2) % ny, i % 2
+            perm.append((i, (((zi + dz) % nz) * ny + (yi + dy) % ny) * 2 + (ci + dc) % 2))
+        return lax.ppermute(a, "wide", perm)
+
+    def send_x(a, k=1):
+        return lax.ppermute(a, "narrow", [(i, (i + k) % nx) for i in range(nx)])
+
+    def send_xc(a):
+        perm = []
+        for i in range(nw):
+            for j in range(nx):
+                perm.append((i * nx + j, (i ^ 1) * nx + (j + 1) % nx))
+        return lax.ppermute(a, ("wide", "narrow"), perm)
+
+    send = {
+        "z": lambda a, k: send_w(a, dz=k),
+        "y": lambda a, k: send_w(a, dy=k),
+        "x": lambda a, k: send_x(a, k),
+    }
+    size = {"z": nz, "y": ny, "x": nx}
+
+    def gather(a, order):
+        for at, dim in enumerate(order):
+            parts = [a] + [send[dim](a, k) for k in range(1, size[dim])]
+            if at == len(order) - 1:
+                return parts
+            a = jnp.stack(parts)
+
+    def pick(flag, a, b):
+        return jnp.where(flag == 0, a, b)
+
+    def in_order(flag, own, oth, axis=0):
+        return pick(
+            flag, jnp.concatenate([own, oth], axis=axis), jnp.concatenate([oth, own], axis=axis)
+        )
+
+    vectors = (query_bias, value_bias, out_bias, up_bias, down_bias, attn_gain, mlp_gain)
+    widths = [piece.shape[0] for piece in vectors]
+    packed = jnp.concatenate(vectors)
+    nv = packed.shape[0]
+    segs = segment_ids[0]
+    vec_x = send_x(jnp.concatenate([packed, segs.astype(BF)]))
+    vec_xc = send_xc(packed)
+
+    def halves(a):
+        return a[:, :grp], a[:, grp:]
+
+    up4 = up_proj.reshape(wr, nj, 2, ffb)
+    qs, ks, vs, os = halves(query_proj), halves(key_proj), halves(value_proj), halves(out_proj)
+    us = (up4[:, :, 0].reshape(wr, ffx), up4[:, :, 1].reshape(wr, ffx))
+    sides = [jnp.concatenate([us[s], os[s], qs[s], ks[s], vs[s]], axis=1) for s in range(2)]
+    keep = pick(c, sides[0], sides[1])
+    give = pick(c, sides[1], sides[0])
+    got = send_w(give, dc=1)
+    vec_c = send_w(packed, dc=1)
+    pair = in_order(c, keep, got)
+    uo = pair[:, : ffx + grp]
+    own_vec = in_order(x, packed[None], vec_x[None, :nv])
+    oth_vec = in_order(x, vec_c[None], vec_xc[None])
+    vec4 = in_order(c, own_vec, oth_vec).reshape(-1)
+    tail_rows = 16
+    vec_block = jnp.pad(vec4, (0, tail_rows * 3 * grp - vec4.shape[0])).reshape(tail_rows, 3 * grp)
+    qkv_block = jnp.concatenate([pair[:, ffx + grp :], vec_block], axis=0)
+
+    wa = gather(qkv_block, "zy")
+    frames_oth = send_x(frames)
+    wb = [send_w(a[:, : 2 * wr], dc=1) for a in wa]
+    dout_par = send_w(out_grad, dc=1)
+    uo_all = gather(uo, "xzy")
+    down_all = gather(down_proj, "zyx")
+    wo_par = send_w(jnp.stack([a[:, :, :, ffx:] for a in uo_all]), dc=1)
+
+    count = nw * nx * nv // nb
+    table = jnp.stack([a[:, 2 * wr :].reshape(nz, -1)[:, :count] for a in wa]).reshape(nb, count)
+    here = jnp.arange(nb)
+    back = lax.rem(y + ny - here % ny, ny) * nz + lax.rem(z + nz - here // ny, nz)
+    table = dot((back[:, None] == here[None, :]).astype(BF), table).reshape(nw * nx, nv)
+    full_vec = []
+    offset = 0
+    for width in widths:
+        full_vec.append(table[:, offset : offset + width].reshape(1, -1))
+        offset = offset + width
+    b_query, b_value, b_out, b_up, b_down, g_attn, g_mlp = full_vec
+
+    def own_heads(v):
+        mine = lax.dynamic_slice(v, (0, x * 2 * grp), (1, 2 * grp))
+        return pick(c, mine, jnp.concatenate([mine[:, grp:], mine[:, :grp]], axis=1))
+
+    qb, vb = own_heads(b_query), own_heads(b_value)
+    ub = lax.dynamic_index_in_dim(b_up.reshape(nb, 2, ffb), c, axis=1)
+
+    sc_at = jnp.arange(5, dtype=jnp.int32)
+    sc = jnp.where(sc_at == 0, z, jnp.where(sc_at == 1, y, jnp.where(sc_at == 2, c, x)))
+    sc = jnp.where(sc_at == 4, row_length[0], sc).astype(jnp.int32)
+
+    seg_row = in_order(x, segs, vec_x[nv:].astype(jnp.int32))
+    segc, segr = seg_row.reshape(rows, 1), seg_row.reshape(1, rows)
+
+    rb = min(256, m)
+    steps = rows // rb
+    per = m // rb
+    wspec = whole((nz, 2 * wr, 3 * grp))
+    dims = dict(nz=nz, ny=ny, blk=blk)
+    row_own = pl.BlockSpec((rb, d), lambda i, sc: (i % per, 0))
+    wide_row = pl.BlockSpec((rb, d), lambda i, sc: (i, 0))
+    heads_row = pl.BlockSpec((rb, 2 * grp), lambda i, sc: (i, 0))
+    q, k, v, act_one = call(
+        functools.partial(qkv_kernel, grp=grp, **dims),
+        sc,
+        (frames, frames_oth, g_attn, qb, vb, wa[0], wa[1], wb[0], wb[1]),
+        (steps,),
+        [row_own, row_own, whole((1, d)), whole((1, 2 * grp)), whole((1, 2 * grp))] + [wspec] * 4,
+        [heads_row, heads_row, heads_row, wide_row],
+        [sds((rows, 2 * grp), BF)] * 3 + [sds((rows, d), BF)],
+        [pltpu.VMEM((rb, d), BF)],
+    )
+
+    pairs = 2 * grp // 128
+    qblk = min(256, rows)
+    rel_pair = pl.BlockSpec((rows, 128), lambda i, sc: (0, i))
+
+    def abs_map(i, sc):
+        return (0, lax.rem(i + sc[2] * (pairs // 2), pairs))
+
+    abs_pair = pl.BlockSpec((rows, 128), abs_map)
+    ctx, lse = call(
+        functools.partial(attn_kernel, qb=qblk),
+        sc,
+        (segc, segr, q, k, v),
+        (pairs,),
+        [whole((rows, 1)), whole((1, rows)), rel_pair, rel_pair, rel_pair],
+        [abs_pair, whole((rows, 128))],
+        [sds((rows, 2 * grp), BF), sds((rows, 128), F32)],
+        [pltpu.VMEM((rows, rows), F32)],
+    )
+
+    def split_rows(a):
+        return (
+            lax.dynamic_slice(a, (x * m, 0), (m, a.shape[1])),
+            lax.dynamic_slice(a, ((1 - x) * m, 0), (m, a.shape[1])),
+        )
+
+    ctx_own, ctx_give = split_rows(ctx)
+    ctx_oth = send_x(ctx_give)
+
+    ospec = pl.BlockSpec(
+        (nz, nx, blk, wc), lambda i, sc: (0, 0, 0, ffx // wc), pipeline_mode=pl.Buffered(1)
+    )
+    obspec = whole((2, nz, nx, blk, wc))
+    fsteps = m // rb
+    half_row = pl.BlockSpec((rb, 2 * grp), lambda i, sc: (i, 0))
+    ctx_rel, mid, act_own = call(
+        functools.partial(out_kernel, nx=nx, wc=wc, **dims),
+        sc,
+        (ctx_own, ctx_oth, frames, b_out, g_mlp, uo_all[0], uo_all[1], wo_par),
+        (fsteps,),
+        [half_row, half_row, wide_row, whole((1, d)), whole((1, d)), ospec, ospec, obspec],
+        [wide_row, wide_row, wide_row],
+        [sds((m, d), BF), sds((m, d), F32), sds((m, d), BF)],
+        [pltpu.VMEM((rb, d), BF), pltpu.VMEM((rb, d), F32)],
+    )
+    act_par = send_w(act_own, dc=1)
+
+    def up_map(t, sc):
+        zy = place(sc, t, nz, ny)
+        xrel = lax.rem(sc[3] + nx - zy // nj, nx)
+        return xrel, zy % nj
+
+    def up_in(t, sc):
+        xrel, j = up_map(t, sc)
+        return (0, xrel, 0, j)
+
+    def up_out(t, sc):
+        xrel, j = up_map(t, sc)
+        return (xrel, 0, j)
+
+    upspec = pl.BlockSpec((nz, 1, blk, ffb), up_in)
+    dnspec = pl.BlockSpec((1, 1, ffb, hw), lambda t, sc: (t // nz, t % nz, 0, 0))
+    bspec = pl.BlockSpec((1, 1, ffb), lambda t, sc: (place(sc, t, nz, ny), 0, 0))
+    kk = nz * blk
+    bo, bo_give, da, da_give, gu, gu_give, gd, gd_give, g_up = call(
+        mlp_kernel,
+        sc,
+        (act_own, act_par, out_grad, dout_par, ub, uo_all[0], uo_all[1], down_all[0], down_all[1]),
+        (nb,),
+        [whole((m, d))] * 4 + [bspec, upspec, upspec, dnspec, dnspec],
+        [whole((m, d))] * 4
+        + [pl.BlockSpec((1, kk, ffb), up_out)] * 2
+        + [pl.BlockSpec((1, ffb, hw), lambda t, sc: (t, 0, 0))] * 2
+        + [bspec],
+        [sds((m, d), F32), sds((m, d), BF), sds((m, d), F32), sds((m, d), BF)]
+        + [sds((nx, kk, nj * ffb), BF)] * 2
+        + [sds((nb, ffb, hw), BF)] * 2
+        + [sds((nb, 1, ffb), F32)],
+        [
+            pltpu.VMEM((2 * m, d), BF),
+            pltpu.VMEM((d, 2 * m), BF),
+            pltpu.VMEM((2 * m, d), BF),
+            pltpu.VMEM((2 * m, d), F32),
+            pltpu.VMEM((2 * m, d), F32),
+        ],
+    )
+    da_got = send_w(da_give, dc=1)
+    bo_got = send_w(bo_give, dc=1)
+    gd_got = send_x(gd_give)
+    gu_got = send_w(gu_give, dy=1)
+
+    gblk, dmid, dctx_own, dctx_give, wo, wo_give, vec_mid = call(
+        functools.partial(mid_kernel, nx=nx, wc=wc, **dims),
+        sc,
+        (
+            da, da_got, bo, bo_got, mid, out_grad, g_mlp, b_down, ctx_rel,
+            uo_all[0], uo_all[1], wo_par,
+        ),
+        (fsteps,),
+        [wide_row] * 6 + [whole((1, d)), whole((1, d)), wide_row, ospec, ospec, obspec],
+        [wide_row, wide_row, half_row, half_row, whole((d, nx * wc)), whole((d, nx * wc))]
+        + [whole((8, d))],
+        [sds((m, d), BF), sds((m, d), F32), sds((m, 2 * grp), BF), sds((m, 2 * grp), BF)]
+        + [sds((d, nx * wc), BF)] * 2
+        + [sds((8, d), F32)],
+        [
+            pltpu.VMEM((rb, d), F32),
+            pltpu.VMEM((rb, d), BF),
+            pltpu.VMEM((rb, d), BF),
+            pltpu.VMEM((d, nx * wc), F32),
+            pltpu.VMEM((d, nx * wc), F32),
+        ],
+    )
+    block_out = gblk
+    dctx_oth = send_x(dctx_give)
+    wo_got = send_w(wo_give, dc=1)
+    dctx = in_order(x, dctx_own, dctx_oth)
+
+    dq, dk, dv = call(
+        functools.partial(attn_back_kernel, qb=qblk),
+        sc,
+        (segc, segr, q, k, v, dctx, lse),
+        (pairs,),
+        [whole((rows, 1)), whole((1, rows)), rel_pair, rel_pair, rel_pair, abs_pair]
+        + [whole((rows, 128))],
+        [rel_pair] * 3,
+        [sds((rows, 2 * grp), BF)] * 3,
+        [
+            pltpu.VMEM((rows, rows), F32),
+            pltpu.VMEM((rows, 128), F32),
+            pltpu.VMEM((rows, 128), F32),
+        ],
+    )
+
+    gd0 = [add_low(gd[e : e + nz], gd_got[e : e + nz]).astype(BF) for e in range(0, nb, nz)]
+    gd1 = add_low(gd0[0], *[send_w(gd0[e], dy=-e) for e in range(1, ny)]).astype(BF)
+    down_grad = add_low(gd1[0], *[send_w(gd1[e], dz=-e) for e in range(1, nz)])
+
+    gu = gu.reshape(nx, nz, blk, ffx)
+    gu_got = gu_got.reshape(nx, nz, blk, ffx)
+    gu0 = [add_low(gu[:, e], gu_got[:, e]).astype(BF) for e in range(nz)]
+    gu1 = add_low(gu0[0], *[send_w(gu0[e], dz=-e) for e in range(1, nz)]).astype(BF)
+    gu2 = add_low(gu1[0], *[send_x(gu1[e], -e) for e in range(1, nx)])
+
+    go0 = add_low(wo, wo_got).astype(BF)
+    go1 = add_low(go0[:, :wc], send_x(go0[:, wc:])).reshape(nb, blk, wc)
+
+    def abs_rows(i, sc):
+        return (lax.rem(i + (1 - sc[3]) * per, 2 * per), 0)
+
+    order_row = pl.BlockSpec((rb, 2 * grp), abs_rows)
+    order_wide = pl.BlockSpec((rb, d), abs_rows)
+    late = pl.BlockSpec((rb, d), lambda i, sc: (jnp.maximum(i - per, 0), 0))
+    early = pl.BlockSpec((rb, d), lambda i, sc: (jnp.minimum(i, per - 1), 0))
+    dact, dact_give, wg, wg_give, vec_one = call(
+        functools.partial(dact_kernel, grp=grp, **dims),
+        sc,
+        (dq, dk, dv, frames, frames_oth, g_attn, act_one, wa[0], wa[1], wb[0], wb[1]),
+        (steps,),
+        [order_row] * 3 + [late, early, whole((1, d)), order_wide] + [wspec] * 4,
+        [late, early, whole((d, 3 * grp)), whole((d, 3 * grp)), whole((8, d))],
+        [sds((m, d), F32), sds((m, d), BF)] + [sds((d, 3 * grp), BF)] * 2 + [sds((8, d), F32)],
+        [pltpu.VMEM((rb, d), F32), pltpu.VMEM((d, 6 * grp), F32)],
+    )
+    dact_got = send_x(dact_give)
+    wg_got = send_w(wg_give, dc=1)
+
+    def other_heads(v):
+        mine = pick(c, v, jnp.concatenate([v[:, grp:], v[:, :grp]], axis=1))
+        return in_order(x, mine, jnp.zeros_like(mine), axis=1)
+
+    core_at = lax.broadcasted_iota(jnp.int32, (nb, 2, ffb), 1)
+    up_bias_grad = jnp.where(core_at == c, g_up.reshape(nb, 1, ffb), 0.0)
+    small = (
+        other_heads(vec_one[1:2, : 2 * grp]),
+        other_heads(vec_one[2:3, : 2 * grp]),
+        vec_mid[1:2],
+        up_bias_grad,
+        vec_mid[2:3],
+        vec_one[0:1],
+        vec_mid[0:1],
+    )
+    vg = jnp.concatenate([g.reshape(nw * nx, width) for g, width in zip(small, widths)], axis=1)
+    vg = vg + send_w(vg, dc=1)
+    vg = vg + send_x(vg)
+    vg = vg + sum(send_w(vg, dy=e) for e in range(1, ny))
+    vg = vg + sum(send_w(vg, dz=e) for e in range(1, nz))
+    flat = lax.dynamic_slice(vg, (w * nx + x, 0), (1, nv)).reshape(-1)
+    vec_out = []
+    offset = 0
+    for width in widths:
+        vec_out.append(flat[offset : offset + width])
+        offset = offset + width
+
+    gq0 = add_low(wg, wg_got).reshape(nb, blk, 3 * grp)
+    gq0 = jnp.concatenate([gq0, go1], axis=2).astype(BF)
+    gq1 = [gq0[e : e + nz] for e in range(0, nb, nz)]
+    gq1 = add_low(gq1[0], *[send_w(gq1[e], dy=-e) for e in range(1, ny)]).astype(BF)
+    gq2 = add_low(gq1[0], *[send_w(gq1[e], dz=-e) for e in range(1, nz)])
+
+    last = jnp.concatenate([gu2, gq2], axis=1)
+    mine = lax.dynamic_slice(last, (c * wr, 0), (wr, last.shape[1]))
+    theirs = send_w(
+        lax.dynamic_slice(last, ((1 - c) * wr, 0), (wr, last.shape[1])).astype(BF), dc=1
+    ).astype(F32)
+    sides = (pick(c, mine, theirs), pick(c, theirs, mine))
+    up_grad = jnp.concatenate(
+        [s[:, :ffx].reshape(wr, nj, 1, ffb) for s in sides], axis=2
+    ).reshape(wr, 2 * ffx)
+    weights = []
+    for at in range(4):
+        lo = ffx + at * grp
+        weights.append(jnp.concatenate([s[:, lo : lo + grp] for s in sides], axis=1))
+
+    rowspec = pl.BlockSpec((rb, d), lambda i, sc: (i, 0))
+    frames_grad = call(
+        last_kernel,
+        sc,
+        (dact, dact_got, dmid, frames, g_attn),
+        (fsteps,),
+        [rowspec] * 4 + [whole((1, d))],
+        rowspec,
+        sds((m, d), BF),
+    )
+    return (block_out, frames_grad, *weights, up_grad, down_grad, *vec_out)
 
 
 def product(left, right):
@@ -374,9 +1099,23 @@
     )
 
 
+def plan(mesh):
+    nw, nx = mesh.shape["wide"], mesh.shape["narrow"]
+    if nx != 2 or nw % 4:
+        return None
+    return nw // 4, 2, nx
+
+
+def either(parts, *args):
+    d = args[0].shape[1]
+    if parts is None or (d // (parts[0] * parts[1])) % 128 or args[3].shape[1] % 256:
+        return body(*args)
+    return fast_body(*parts, *args)
+
+
 def solution(mesh):
     return jax.shard_map(
-        body,
+        functools.partial(either, plan(mesh)),
         mesh=mesh,
         in_specs=(
             P(("wide", "narrow"), None),

time: 1290 us -> 551 us (0.43)
  waiting for transfers between devices: 871 us -> 281 us
  matrix products: 182 us -> 0.83 us
  Pallas kernels: 0 us -> 137 us
  blocking collectives: 132 us -> 0 us
  starting transfers between devices: 1.73 us -> 63.8 us
  other arithmetic: 46.1 us -> 30.8 us
  between operations: 16.6 us -> 2.56 us
    reduce_scatter x15 -> x0, waiting for transfers between devices: 628 us -> none  [the longest x1 101 us: body(): lax.psum_scatter(up_grad.astype(jnp.bfloat16), 'narrow', scatter_dimensio...]
    ppermute x0 -> x53, waiting for transfers between devices: none -> 281 us  [the longest x41 218 us: send_w(): return lax.ppermute(a, 'wide', perm)]
    all_gather x8 -> x0, waiting for transfers between devices: 242 us -> none  [the longest x1 70.5 us: gather_params(): lax.all_gather(inner[4], 'wide', axis=0, tiled=True)]
    dot_general x42 -> x1, matrix products: 182 us -> 0.83 us  [dot(): return jnp.dot(left, right, preferred_element_type=F32)]
    pallas_call x0 -> x8, Pallas kernels: none -> 137 us  [call(): pl.pallas_call(kernel, grid_spec=spec, out_shape=out_shape, compiler_para...]
    all_gather x8 -> x0, blocking collectives: 66 us -> none  [the longest x1 21.9 us: gather_params(): lax.all_gather(inner[6], 'wide', axis=0, tiled=True)]
    unnamed x2 -> x0, blocking collectives: 66 us -> none
    ppermute x0 -> x53, starting transfers between devices: none -> 63.8 us  [the longest x41 53.5 us: send_w(): return lax.ppermute(a, 'wide', perm)]
  transfers between devices with their start and end apart: 23 -> 53, of which waited for: 18 -> 26; matrix products, arithmetic and copies ran while one was open for 15% -> 9% of each run, Pallas kernels for 0% -> 18%
where the time goes in v1:
time: 551 us; the launch traced here: 546 us
  waiting for transfers between devices  281 us (51%)
  Pallas kernels  137 us (25%)
  starting transfers between devices  63.8 us (12%)
  other arithmetic  30.8 us (6%)
  local copies, waits for them, and re-layouts  30 us (5%)
    ppermute x41, waiting for transfers between devices, send_w(): return lax.ppermute(a, 'wide', perm)  218 us
    pallas_call x8, Pallas kernels, call(): pl.pallas_call(kernel, grid_spec=spec, out_shape=out_shape, compiler_para...  137 us
    ppermute x11, waiting for transfers between devices, send_x(): return lax.ppermute(a, 'narrow', [(i, (i + k) % nx) for i in range(nx)])  63.3 us
    ppermute x41, starting transfers between devices, send_w(): return lax.ppermute(a, 'wide', perm)  53.5 us
  transfers between devices with their start and end apart: 53, of which 26 were waited for; matrix products, arithmetic and copies ran while one was open for 9% of the time, Pallas kernels for 18%

profile of v1, /device:TPU:0, one launch (start us, length us, event | category | flops | bytes accessed | tf_op | source)
XLA Modules:
  0.0 546.3 jit_solution(3273709876953845289)
XLA Ops:
  0.8 4.9 concatenate.151
  21.0 8.9 %collective-permute-done.12 = bf16[128,1280]{1,0:T(8,128)(2,1)S(1)} collective-permute-done((bf16[128,1280]{1,0:T(8,128)(2,1)S(1)}, bf16[128,1280]{1,0:T(8,128)(2,1)S(1)}, u32[]{:S(2)}, u32[]{:S(2)}) %collective-permute-start.12) | collective-permute-done | bytes 327712 | tf_op jit(solution)/shard_map/ppermute | solution.py:401
  38.0 39.0 %collective-permute-done.14 = bf16[2,128,1280]{2,1,0:T(8,128)(2,1)S(1)} collective-permute-done((bf16[2,128,1280]{2,1,0:T(8,128)(2,1)}, bf16[2,128,1280]{2,1,0:T(8,128)(2,1)S(1)}, u32[]{:S(2)}, u32[]{:S(2)}) %collective-permute-start.14) | collective-permute-done | bytes 655392 | tf_op jit(solution)/shard_map/ppermute | solution.py:398
  77.0 22.0 %collective-permute-start.5 = (bf16[144,768]{1,0:T(8,128)(2,1)S(1)}, bf16[144,768]{1,0:T(8,128)(2,1)S(1)}, u32[]{:S(2)}, u32[]{:S(2)}) collective-permute-start(bf16[144,768]{1,0:T(8,128)(2,1)S(1)} %get-tuple-element.116), channel_id=1, source_target_pairs={{0,8},{2,10},{4,12},{6,14},{8,16},{10,18},{12,20},{14,22},{16,24},... | collective-permute-start | bytes 663560 | tf_op jit(solution)/shard_map/ppermute | solution.py:398
  102.0 7.8 %collective-permute-done.21 = bf16[256,512]{1,0:T(8,128)(2,1)S(1)} collective-permute-done((bf16[256,512]{1,0:T(8,128)(2,1)S(1)}, bf16[256,512]{1,0:T(8,128)(2,1)S(1)}, u32[]{:S(2)}, u32[]{:S(2)}) %collective-permute-start.21) | collective-permute-done | bytes 262176 | tf_op jit(solution)/shard_map/ppermute | solution.py:398
  122.7 69.3 %collective-permute-done.23 = bf16[4,256,512]{2,1,0:T(8,128)(2,1)S(1)} collective-permute-done((bf16[4,256,512]{2,1,0:T(8,128)(2,1)S(1)}, bf16[4,256,512]{2,1,0:T(8,128)(2,1)S(1)}, u32[]{:S(2)}, u32[]{:S(2)}) %collective-permute-start.23) | collective-permute-done | bytes 1048608 | tf_op jit(solution)/shard_map/ppermute | solution.py:398
  194.0 15.8 %collective-permute-done.8.wa1 = bf16[4,144,768]{2,1,0:T(8,128)(2,1)S(1)} collective-permute-done((bf16[4,144,768]{2,1,0:T(8,128)(2,1)S(1)}, bf16[4,144,768]{2,1,0:T(8,128)(2,1)S(1)}, u32[]{:S(2)}, u32[]{:S(2)}) %collective-permute-start.8) | collective-permute-done | bytes 884768 | tf_op jit(solution)/shard_map/ppermute | solution.py:398
  219.3 9.5 %shard_map.280 = (bf16[1024,512]{1,0:T(8,128)(2,1)}, bf16[1024,512]{1,0:T(8,128)(2,1)}, bf16[1024,512]{1,0:T(8,128)(2,1)}, bf16[1024,1024]{1,0:T(8,128)(2,1)}) custom-call(s32[5]{0:T(128)} %compare_select_fusion.7.sc, bf16[512,1024]{1,0:T(8,128)(2,1)} %fr.3, bf16[512,1024]{1,0:T(8,128)(2,1)} %collective-permute-done.1.oth, f32[1,1024]{1,0:T(1,128)} %reshape.302.gain, ...), custom_call_target="tpu_custom_call" | custom-call | tf_op jit(solution)/shard_map/pallas_call | solution.py:49
  228.9 20.4 %shard_map.281 = (bf16[1024,512]{1,0:T(8,128)(2,1)}, f32[1024,128]{1,0:T(8,128)}) custom-call(s32[5]{0:T(128)} %compare_select_fusion.7.sc, s32[1024,1]{1,0:T(8,128)} %broadcast_select_fusion.2.segc, s32[1,1024]{1,0:T(1,128)} %broadcast_select_fusion.6.segr, bf16[1024,512]{1,0:T(8,128)(2,1)} %get-tuple-element.48.q, bf16[1024,512]{1,0:T(8,128)(2,1)} %get-tuple-element.49.k, ...), custom_call_target="tpu_custom_call" | custom-call | tf_op jit(solution)/shard_map/pallas_call | solution.py:49
  253.5 12.3 %collective-permute-done.11.coth = bf16[512,512]{1,0:T(8,128)(2,1)} collective-permute-done((bf16[512,512]{1,0:T(8,128)(2,1)}, bf16[512,512]{1,0:T(8,128)(2,1)}, u32[]{:S(2)}, u32[]{:S(2)}) %collective-permute-start.11) | collective-permute-done | bytes 524320 | tf_op jit(solution)/shard_map/ppermute | solution.py:401
  266.8 6.1 %shard_map.282 = (bf16[512,1024]{1,0:T(8,128)(2,1)}, f32[512,1024]{1,0:T(8,128)}, bf16[512,1024]{1,0:T(8,128)(2,1)}) custom-call(s32[5]{0:T(128)} %compare_select_fusion.7.sc, bf16[512,512]{1,0:T(8,128)(2,1)} %get-tuple-element.100.cown, bf16[512,512]{1,0:T(8,128)(2,1)} %collective-permute-done.11.coth, bf16[512,1024]{1,0:T(8,128)(2,1)} %fr.3, ...), custom_call_target="tpu_custom_call" | custom-call | tf_op jit(solution)/shard_map/pallas_call | solution.py:49
  276.7 41.3 %shard_map.283 = (f32[512,1024]{1,0:T(8,128)}, bf16[512,1024]{1,0:T(8,128)(2,1)}, f32[512,1024]{1,0:T(8,128)}, bf16[512,1024]{1,0:T(8,128)(2,1)}, bf16[2,512,102...) custom-call(s32[5]{0:T(128)} %compare_select_fusion.7.sc, ...), custom_call_target="tpu_custom_call" | custom-call | tf_op jit(solution)/shard_map/pallas_call | solution.py:49
  323.4 11.8 %shard_map.284 = (bf16[512,1024]{1,0:T(8,128)(2,1)}, f32[512,1024]{1,0:T(8,128)}, bf16[512,512]{1,0:T(8,128)(2,1)}, bf16[512,512]{1,0:T(8,128)(2,1)}, bf16[1024,...) custom-call(s32[5]{0:T(128)} %compare_select_fusion.7.sc, f32[512,1024]{1,0:T(8,128)} %get-tuple-element.53.da, ...), custom_call_target="tpu_custom_call" | custom-call | tf_op jit(solution)/shard_map/pallas_call | solution.py:49
  338.6 11.7 %collective-permute-done.27 = bf16[512,512]{1,0:T(8,128)(2,1)S(1)} collective-permute-done((bf16[512,512]{1,0:T(8,128)(2,1)}, bf16[512,512]{1,0:T(8,128)(2,1)S(1)}, u32[]{:S(2)}, u32[]{:S(2)}) %collective-permute-start.27) | collective-permute-done | bytes 524320 | tf_op jit(solution)/shard_map/ppermute | solution.py:401
  352.8 27.5 %shard_map.285 = (bf16[1024,512]{1,0:T(8,128)(2,1)}, bf16[1024,512]{1,0:T(8,128)(2,1)}, bf16[1024,512]{1,0:T(8,128)(2,1)}) custom-call(s32[5]{0:T(128)} %compare_select_fusion.7.sc, s32[1024,1]{1,0:T(8,128)} %broadcast_select_fusion.2.segc, s32[1,1024]{1,0:T(1,128)} %broadcast_select_fusion.6.segr, bf16[1024,512]{1,0:T(8,128)(2,1)} %get-tuple-element.48.q, ...), custom_call_target="tpu_custom_call" | custom-call | tf_op jit(solution)/shard_map/pallas_call | solution.py:49
  380.3 15.7 %shard_map.286 = (f32[512,1024]{1,0:T(8,128)}, bf16[512,1024]{1,0:T(8,128)(2,1)}, bf16[1024,768]{1,0:T(8,128)(2,1)}, bf16[1024,768]{1,0:T(8,128)(2,1)}, f32[8,1024]{1,0:T(8,128)}) custom-call(s32[5]{0:T(128)} %compare_select_fusion.7.sc, bf16[1024,512]{1,0:T(8,128)(2,1)} %get-tuple-element.63.dq, bf16[1024,512]{1,0:T(8,128)(2,1)} %get-tuple-element.64.dk, ...), custom_call_target="tpu_custom_call" | custom-call | tf_op jit(solution)/shard_map/pallas_call | solution.py:49
  412.7 5.0 collective-permute-done.51
  417.7 5.9 %collective-permute-done.50 = f32[32,320]{1,0:T(8,128)S(1)} collective-permute-done((f32[32,320]{1,0:T(8,128)S(1)}, f32[32,320]{1,0:T(8,128)S(1)}, u32[]{:S(2)}, u32[]{:S(2)}) %collective-permute-start.50) | collective-permute-done | bytes 40992 | tf_op jit(solution)/shard_map/ppermute | solution.py:398
  431.2 23.6 %collective-permute-done.36 = bf16[1024,256]{1,0:T(8,128)(2,1)S(1)} collective-permute-done((bf16[1024,256]{1,0:T(8,128)(2,1)S(1)}, bf16[1024,256]{1,0:T(8,128)(2,1)S(1)}, u32[]{:S(2)}, u32[]{:S(2)}) %collective-permute-start.36) | collective-permute-done | bytes 524320 | tf_op jit(solution)/shard_map/ppermute | solution.py:401
  460.3 9.7 %collective-permute-done.31 = bf16[2,128,1024]{2,1,0:T(8,128)(2,1)S(1)} collective-permute-done((bf16[2,128,1024]{2,1,0:T(8,128)(2,1)S(1)}, bf16[2,128,1024]{2,1,0:T(8,128)(2,1)S(1)}, u32[]{:S(2)}, u32[]{:S(2)}) %collective-permute-start.31) | collective-permute-done | bytes 524320 | tf_op jit(solution)/shard_map/ppermute | solution.py:398
  473.3 4.8 shard_map.287
  478.2 18.8 %collective-permute-done.37 = bf16[4,128,1024]{2,1,0:T(8,128)(2,1)} collective-permute-done((bf16[4,128,1024]{2,1,0:T(8,128)(2,1)}, bf16[4,128,1024]{2,1,0:T(8,128)(2,1)}, u32[]{:S(2)}, u32[]{:S(2)}) %collective-permute-start.37) | collective-permute-done | bytes 1048608 | tf_op jit(solution)/shard_map/ppermute | solution.py:398
  515.0 17.8 %collective-permute-done.39 = bf16[128,1024]{1,0:T(8,128)(2,1)S(1)} collective-permute-done((bf16[128,1024]{1,0:T(8,128)(2,1)S(1)}, bf16[128,1024]{1,0:T(8,128)(2,1)S(1)}, u32[]{:S(2)}, u32[]{:S(2)}) %collective-permute-start.39) | collective-permute-done | bytes 262176 | tf_op jit(solution)/shard_map/ppermute | solution.py:398
  533.1 7.1 %collective-permute-done.45 = bf16[256,512]{1,0:T(8,128)(2,1)S(1)} collective-permute-done((bf16[256,512]{1,0:T(8,128)(2,1)S(1)}, bf16[256,512]{1,0:T(8,128)(2,1)S(1)}, u32[]{:S(2)}, u32[]{:S(2)}) %collective-permute-start.45) | collective-permute-done | bytes 262176 | tf_op jit(solution)/shard_map/ppermute | solution.py:398
  (293 shorter events, 127.3 us)
Async XLA Ops:
  10.3 91.0 %collective-permute-start.22 = (bf16[256,512]{1,0:T(8,128)(2,1)}, bf16[256,512]{1,0:T(8,128)(2,1)}, u32[]{:S(2)}, u32[]{:S(2)}) collective-permute-start(bf16[256,512]{1,0:T(8,128)(2,1)} %param.25), channel_id=1, source_target_pairs={{0,24},{2,26},{4,28},{6,30},{8,0},{10,2},{12,4},{14,6},{16,8},{18,... | collective-permute-start | bytes 786440 | tf_op jit(solution)/shard_map/ppermute | solution.py:398
  30.8 46.2 %collective-permute-start.14 = (bf16[2,128,1280]{2,1,0:T(8,128)(2,1)}, bf16[2,128,1280]{2,1,0:T(8,128)(2,1)S(1)}, u32[]{:S(2)}, u32[]{:S(2)}) collective-permute-start(bf16[2,128,1280]{2,1,0:T(8,128)(2,1)} %get-tuple-element.102), channel_id=1, source_target_pairs={{0,16},{2,18},{4,20},{6,22},{8,24},{10,26},{12,28},{14,30},{16,0},... | collective-permute-start | bytes 1966088 | tf_op jit(solution)/shard_map/ppermute | solution.py:398
  31.6 45.4 %collective-permute-start.13 = (bf16[2,128,1280]{2,1,0:T(8,128)(2,1)}, bf16[2,128,1280]{2,1,0:T(8,128)(2,1)}, u32[]{:S(2)}, u32[]{:S(2)}) collective-permute-start(bf16[2,128,1280]{2,1,0:T(8,128)(2,1)} %get-tuple-element.102), channel_id=1, source_target_pairs={{0,8},{2,10},{4,12},{6,14},{8,16},{10,18},{12,20},{14,22},{16,24},... | collective-permute-start | bytes 1966088 | tf_op jit(solution)/shard_map/ppermute | solution.py:398
  33.2 65.8 %collective-permute-start.15 = (bf16[2,128,1280]{2,1,0:T(8,128)(2,1)}, bf16[2,128,1280]{2,1,0:T(8,128)(2,1)}, u32[]{:S(2)}, u32[]{:S(2)}) collective-permute-start(bf16[2,128,1280]{2,1,0:T(8,128)(2,1)} %get-tuple-element.102), channel_id=1, source_target_pairs={{0,24},{2,26},{4,28},{6,30},{8,0},{10,2},{12,4},{14,6},{16,8},{18,... | collective-permute-start | bytes 1966088 | tf_op jit(solution)/shard_map/ppermute | solution.py:398
  37.6 72.1 %collective-permute-start.21 = (bf16[256,512]{1,0:T(8,128)(2,1)S(1)}, bf16[256,512]{1,0:T(8,128)(2,1)S(1)}, u32[]{:S(2)}, u32[]{:S(2)}) collective-permute-start(bf16[256,512]{1,0:T(8,128)(2,1)S(1)} %copy-done.18), channel_id=1, source_target_pairs={{0,16},{2,18},{4,20},{6,22},{8,24},{10,26},{12,28},{14,30},{16,0},... | collective-permute-start | bytes 786440 | tf_op jit(solution)/shard_map/ppermute | solution.py:398
  77.0 37.4 %collective-permute-start.6 = (bf16[144,768]{1,0:T(8,128)(2,1)S(1)}, bf16[144,768]{1,0:T(8,128)(2,1)S(1)}, u32[]{:S(2)}, u32[]{:S(2)}) collective-permute-start(bf16[144,768]{1,0:T(8,128)(2,1)S(1)} %get-tuple-element.116), channel_id=1, source_target_pairs={{0,16},{2,18},{4,20},{6,22},{8,24},{10,26},{12,28},{14,30},{16,0},... | collective-permute-start | bytes 663560 | tf_op jit(solution)/shard_map/ppermute | solution.py:398
  77.0 38.9 %collective-permute-start.5 = (bf16[144,768]{1,0:T(8,128)(2,1)S(1)}, bf16[144,768]{1,0:T(8,128)(2,1)S(1)}, u32[]{:S(2)}, u32[]{:S(2)}) collective-permute-start(bf16[144,768]{1,0:T(8,128)(2,1)S(1)} %get-tuple-element.116), channel_id=1, source_target_pairs={{0,8},{2,10},{4,12},{6,14},{8,16},{10,18},{12,20},{14,22},{16,24},... | collective-permute-start | bytes 663560 | tf_op jit(solution)/shard_map/ppermute | solution.py:398
  101.4 117.9 %collective-permute-start.1 = (bf16[512,1024]{1,0:T(8,128)(2,1)}, bf16[512,1024]{1,0:T(8,128)(2,1)}, u32[]{:S(2)}, u32[]{:S(2)}) collective-permute-start(bf16[512,1024]{1,0:T(8,128)(2,1)} %fr.3), channel_id=1, source_target_pairs={{0,1},{1,0},{2,3},{3,2},{4,5},{5,4},{6,7},{7,6},{8,9},{9,8},{10,11... | collective-permute-start | bytes 3145736 | tf_op jit(solution)/shard_map/ppermute | solution.py:401
  109.8 104.9 %collective-permute-start.16 = (bf16[4,2,128,1280]{3,2,1,0:T(8,128)(2,1)S(1)}, bf16[4,2,128,1280]{3,2,1,0:T(8,128)(2,1)}, u32[]{:S(2)}, u32[]{:S(2)}) collective-permute-start(bf16[4,2,128,1280]{3,2,1,0:T(8,128)(2,1)S(1)} %pad_maximum_fusion.wa0.up0), channel_id=1, source_target_pairs={{0,4},{2,6},{4,0},{6,2},{8,12},{10,14},{12,8},{14,10},{16,20},{18,... | collective-permute-start | bytes 7864328 | tf_op jit(solution)/shard_map/ppermute | solution.py:398
  114.4 77.5 %collective-permute-start.23 = (bf16[4,256,512]{2,1,0:T(8,128)(2,1)S(1)}, bf16[4,256,512]{2,1,0:T(8,128)(2,1)S(1)}, u32[]{:S(2)}, u32[]{:S(2)}) collective-permute-start(bf16[4,256,512]{2,1,0:T(8,128)(2,1)S(1)} %get-tuple-element.98), channel_id=1, source_target_pairs={{0,4},{2,6},{4,0},{6,2},{8,12},{10,14},{12,8},{14,10},{16,20},{18,... | collective-permute-start | bytes 3145736 | tf_op jit(solution)/shard_map/ppermute | solution.py:398
  119.2 90.7 %collective-permute-start.8 = (bf16[4,144,768]{2,1,0:T(8,128)(2,1)S(1)}, bf16[4,144,768]{2,1,0:T(8,128)(2,1)S(1)}, u32[]{:S(2)}, u32[]{:S(2)}) collective-permute-start(bf16[4,144,768]{2,1,0:T(8,128)(2,1)S(1)} %pad_maximum_fusion.5.wa0), channel_id=1, source_target_pairs={{0,4},{2,6},{4,0},{6,2},{8,12},{10,14},{12,8},{14,10},{16,20},{18,... | collective-permute-start | bytes 2654216 | tf_op jit(solution)/shard_map/ppermute | solution.py:398
  121.8 97.6 %collective-permute-start.9 = (bf16[4,128,768]{2,1,0:T(8,128)(2,1)}, bf16[4,128,768]{2,1,0:T(8,128)(2,1)}, u32[]{:S(2)}, u32[]{:S(2)}) collective-permute-start(bf16[4,128,768]{2,1,0:T(8,128)(2,1)} %slice.386), channel_id=1, source_target_pairs={{0,2},{2,0},{4,6},{6,4},{8,10},{10,8},{12,14},{14,12},{16,18},{18,... | collective-permute-start | bytes 2359304 | tf_op jit(solution)/shard_map/ppermute | solution.py:398
  193.5 80.1 %collective-permute-start.24 = (bf16[2,4,256,512]{3,2,1,0:T(8,128)(2,1)}, bf16[2,4,256,512]{3,2,1,0:T(8,128)(2,1)}, u32[]{:S(2)}, u32[]{:S(2)}) collective-permute-start(bf16[2,4,256,512]{3,2,1,0:T(8,128)(2,1)} %pad_maximum_fusion.1.dn0), channel_id=1, source_target_pairs={{0,1},{1,0},{2,3},{3,2},{4,5},{5,4},{6,7},{7,6},{8,9},{9,8},{10,11... | collective-permute-start | bytes 6291464 | tf_op jit(solution)/shard_map/ppermute | solution.py:401
  216.9 48.9 %collective-permute-start.17 = (bf16[2,4,2,128,256]{4,3,2,1,0:T(8,128)(2,1)}, bf16[2,4,2,128,256]{4,3,2,1,0:T(8,128)(2,1)S(1)}, u32[]{:S(2)}, u32[]{:S(2)}) collective-permute-start(bf16[2,4,2,128,256]{4,3,2,1,0:T(8,128)(2,1)} %pad_maximum_fusion.3), channel_id=1, source_target_pairs={{0,2},{2,0},{4,6},{6,4},{8,10},{10,8},{12,14},{14,12},{16,18},{18,... | collective-permute-start | bytes 3145736 | tf_op jit(solution)/shard_map/ppermute | solution.py:398
  318.6 108.8 %collective-permute-start.29 = (bf16[2,512,1024]{2,1,0:T(8,128)(2,1)}, bf16[2,512,1024]{2,1,0:T(8,128)(2,1)}, u32[]{:S(2)}, u32[]{:S(2)}) collective-permute-start(bf16[2,512,1024]{2,1,0:T(8,128)(2,1)} %get-tuple-element.71), channel_id=1, source_target_pairs={{0,4},{2,6},{4,0},{6,2},{8,12},{10,14},{12,8},{14,10},{16,20},{18,... | collective-permute-start | bytes 6291464 | tf_op jit(solution)/shard_map/ppermute | solution.py:398
  335.9 94.0 %collective-permute-start.42 = (bf16[8,256,512]{2,1,0:T(8,128)(2,1)}, bf16[8,256,512]{2,1,0:T(8,128)(2,1)S(1)}, u32[]{:S(2)}, u32[]{:S(2)}) collective-permute-start(bf16[8,256,512]{2,1,0:T(8,128)(2,1)} %get-tuple-element.77), channel_id=1, source_target_pairs={{0,1},{1,0},{2,3},{3,2},{4,5},{5,4},{6,7},{7,6},{8,9},{9,8},{10,11... | collective-permute-start | bytes 6291464 | tf_op jit(solution)/shard_map/ppermute | solution.py:401
  338.6 85.6 %collective-permute-start.35 = (bf16[1024,512]{1,0:T(8,128)(2,1)}, bf16[1024,512]{1,0:T(8,128)(2,1)}, u32[]{:S(2)}, u32[]{:S(2)}) collective-permute-start(bf16[1024,512]{1,0:T(8,128)(2,1)} %get-tuple-element.75), channel_id=1, source_target_pairs={{0,2},{2,0},{4,6},{6,4},{8,10},{10,8},{12,14},{14,12},{16,18},{18,... | collective-permute-start | bytes 3145736 | tf_op jit(solution)/shard_map/ppermute | solution.py:398
  396.0 59.1 %collective-permute-start.34 = (bf16[1024,768]{1,0:T(8,128)(2,1)}, bf16[1024,768]{1,0:T(8,128)(2,1)}, u32[]{:S(2)}, u32[]{:S(2)}) collective-permute-start(bf16[1024,768]{1,0:T(8,128)(2,1)} %get-tuple-element.73), channel_id=1, source_target_pairs={{0,2},{2,0},{4,6},{6,4},{8,10},{10,8},{12,14},{14,12},{16,18},{18,... | collective-permute-start | bytes 4718600 | tf_op jit(solution)/shard_map/ppermute | solution.py:398
  423.6 49.7 %collective-permute-start.28 = (bf16[512,1024]{1,0:T(8,128)(2,1)}, bf16[512,1024]{1,0:T(8,128)(2,1)}, u32[]{:S(2)}, u32[]{:S(2)}) collective-permute-start(bf16[512,1024]{1,0:T(8,128)(2,1)} %get-tuple-element.68), channel_id=1, source_target_pairs={{0,1},{1,0},{2,3},{3,2},{4,5},{5,4},{6,7},{7,6},{8,9},{9,8},{10,11... | collective-permute-start | bytes 3145736 | tf_op jit(solution)/shard_map/ppermute | solution.py:401
  429.9 40.1 %collective-permute-start.31 = (bf16[2,128,1024]{2,1,0:T(8,128)(2,1)S(1)}, bf16[2,128,1024]{2,1,0:T(8,128)(2,1)S(1)}, u32[]{:S(2)}, u32[]{:S(2)}) collective-permute-start(bf16[2,128,1024]{2,1,0:T(8,128)(2,1)S(1)} %get-tuple-element.87), channel_id=1, source_target_pairs={{0,16},{2,18},{4,20},{6,22},{8,24},{10,26},{12,28},{14,30},{16,0},... | collective-permute-start | bytes 1572872 | tf_op jit(solution)/shard_map/ppermute | solution.py:398
  455.1 47.6 %collective-permute-start.43 = (bf16[4,256,512]{2,1,0:T(8,128)(2,1)}, bf16[4,256,512]{2,1,0:T(8,128)(2,1)}, u32[]{:S(2)}, u32[]{:S(2)}) collective-permute-start(bf16[4,256,512]{2,1,0:T(8,128)(2,1)} %add_convert_fusion.2), channel_id=1, source_target_pairs={{0,4},{2,6},{4,0},{6,2},{8,12},{10,14},{12,8},{14,10},{16,20},{18,... | collective-permute-start | bytes 3145736 | tf_op jit(solution)/shard_map/ppermute | solution.py:398
  459.8 37.2 %collective-permute-start.37 = (bf16[4,128,1024]{2,1,0:T(8,128)(2,1)}, bf16[4,128,1024]{2,1,0:T(8,128)(2,1)}, u32[]{:S(2)}, u32[]{:S(2)}) collective-permute-start(bf16[4,128,1024]{2,1,0:T(8,128)(2,1)} %pad_maximum_fusion.2), channel_id=1, source_target_pairs={{0,4},{2,6},{4,0},{6,2},{8,12},{10,14},{12,8},{14,10},{16,20},{18,... | collective-permute-start | bytes 3145736 | tf_op jit(solution)/shard_map/ppermute | solution.py:398
  502.1 30.7 %collective-permute-start.39 = (bf16[128,1024]{1,0:T(8,128)(2,1)S(1)}, bf16[128,1024]{1,0:T(8,128)(2,1)S(1)}, u32[]{:S(2)}, u32[]{:S(2)}) collective-permute-start(bf16[128,1024]{1,0:T(8,128)(2,1)S(1)} %get-tuple-element.96), channel_id=1, source_target_pairs={{0,16},{2,18},{4,20},{6,22},{8,24},{10,26},{12,28},{14,30},{16,0},... | collective-permute-start | bytes 786440 | tf_op jit(solution)/shard_map/ppermute | solution.py:398
  509.4 30.9 %collective-permute-start.45 = (bf16[256,512]{1,0:T(8,128)(2,1)S(1)}, bf16[256,512]{1,0:T(8,128)(2,1)S(1)}, u32[]{:S(2)}, u32[]{:S(2)}) collective-permute-start(bf16[256,512]{1,0:T(8,128)(2,1)S(1)} %get-tuple-element.93), channel_id=1, source_target_pairs={{0,16},{2,18},{4,20},{6,22},{8,24},{10,26},{12,28},{14,30},{16,0},... | collective-permute-start | bytes 786440 | tf_op jit(solution)/shard_map/ppermute | solution.py:398
  (68 other events, 964.8 us)

commit v2 on v1

--- a/solution.py
+++ b/solution.py
@@ -63,24 +63,32 @@
 
 
 def qkv_kernel(
-    sc, own, oth, gain, qb, vb, wa0, wa1, wb0, wb1, q_o, k_o, v_o, a_o, tmp, *, nz, ny, blk, grp
+    sc, own, oth, gain, qb, vb, wa0, wa1, wb0, wb1, q_o, k_o, v_o, a_o, w, tmp, *, nz, ny, blk, grp
 ):
     i = pl.program_id(0)
     half = pl.num_programs(0) // 2
+    n = q_o.shape[1]
+
+    @pl.when(i == 0)
+    def _():
+        for crel, pair in enumerate(((wa0, wa1), (wb0, wb1))):
+            base = lax.rem(sc[2] + crel, 2) * grp
+            for p in range(nz * ny):
+                rows = ds(place(sc, p, nz, ny) * blk, blk)
+                for k in range(3):
+                    cols = ds(k * n + base, grp)
+                    w[rows, cols] = pair[p // nz][p % nz, :, k * grp : (k + 1) * grp]
+
     mine = i // half == sc[3]
     f = jnp.where(mine, own[...].astype(F32), oth[...].astype(F32))
     r = lax.rsqrt(jnp.mean(f * f, axis=1, keepdims=True) + EPS)
     tmp[...] = (f * r * gain[...]).astype(BF)
     for p in range(nz * ny):
         a_o[:, p * blk : (p + 1) * blk] = tmp[:, ds(place(sc, p, nz, ny) * blk, blk)]
-    k = nz * blk
-    for g, (w0, w1) in enumerate(((wa0, wa1), (wb0, wb1))):
-        res = dot(a_o[:, :k], w0[...].reshape(k, 3 * grp))
-        res = res + dot(a_o[:, k:], w1[...].reshape(k, 3 * grp))
-        lo, hi = g * grp, (g + 1) * grp
-        q_o[:, lo:hi] = (res[:, :grp] + qb[:, lo:hi]).astype(BF)
-        k_o[:, lo:hi] = res[:, grp : 2 * grp].astype(BF)
-        v_o[:, lo:hi] = (res[:, 2 * grp :] + vb[:, lo:hi]).astype(BF)
+    act = tmp[...]
+    q_o[...] = (dot(act, w[:, :n]) + qb[...]).astype(BF)
+    k_o[...] = dot(act, w[:, n : 2 * n]).astype(BF)
+    v_o[...] = (dot(act, w[:, 2 * n : 3 * n]) + vb[...]).astype(BF)
 
 
 def fill_bias(sc, segc, segr, bias, qb):
@@ -122,7 +130,9 @@
         c_o[start:n, :] = jnp.concatenate(outs, axis=1).astype(BF)
 
 
-def attn_back_kernel(sc, segc, segr, q, k, v, d, l, dq_o, dk_o, dv_o, bias, dks, dvs, *, qb):
+def attn_back_kernel(
+    sc, segc, segr, q, k, v, d, l, dq_o, dk_o, dv_o, qs_o, vs_o, bias, dks, dvs, *, qb
+):
     p = pl.program_id(0)
     total = q.shape[0]
 
@@ -156,36 +166,39 @@
             dks[:n, :] += dkk
             dvs[:n, :] += dvv
     dk_o[...] = dks[...].astype(BF)
-    dv_o[...] = dvs[...].astype(BF)
-
-
-def out_weight(wa, wb, xrel, crel, yrel):
-    block = wa[yrel][:, xrel] if crel == 0 else wb[yrel, :, xrel]
-    return block.reshape(block.shape[0] * block.shape[1], block.shape[2])
+    dvb = dvs[...].astype(BF)
+    dv_o[...] = dvb
+    qs_o[...] = jnp.sum(dq_o[...].astype(F32), axis=0, keepdims=True)
+    vs_o[...] = jnp.sum(dvb.astype(F32), axis=0, keepdims=True)
 
 
 def out_kernel(
-    sc, cown, coth, fr, ob, gain, wa0, wa1, wb, cr_o, mid_o, a_o, cs, ms, *, nz, ny, nx, blk, wc
+    sc, cown, coth, fr, ob, gain, w00, w01, w10, w11, cx_o, mid_o, a_o, w, tmp,
+    *, nz, ny, nx, blk, grp,
 ):
     hw = cown.shape[1]
-    x, c = sc[3], sc[2]
-    cs[:, ds(x * hw, hw)] = cown[...]
-    cs[:, ds((1 - x) * hw, hw)] = coth[...]
-    for p in range(nz * ny):
-        cr_o[:, p * blk : (p + 1) * blk] = cs[:, ds(place(sc, p, nz, ny) * blk, blk)]
-    k = nz * blk
-    for xrel in range(nx):
-        for crel in range(2):
-            acc = dot(cr_o[:, :k], out_weight((wa0, wa1), wb, xrel, crel, 0))
-            acc = acc + dot(cr_o[:, k:], out_weight((wa0, wa1), wb, xrel, crel, 1))
-            base = lax.rem(x + xrel, nx) * 2 + lax.rem(c + crel, 2)
-            ms[:, ds(base * wc, wc)] = acc
-    mid = fr[...].astype(F32) + ms[...] + ob[...]
+    x = sc[3]
+
+    @pl.when(pl.program_id(0) == 0)
+    def _():
+        for xrel, pair in enumerate(((w00, w01), (w10, w11))):
+            for crel, part in enumerate(pair):
+                base = lax.rem(x + xrel, nx) * hw + lax.rem(sc[2] + crel, 2) * grp
+                for p in range(nz * ny):
+                    got = part[p // nz, p % nz]
+                    zy = place(sc, p, nz, ny)
+                    for side in range(2):
+                        rows = ds(zy * blk + side * (blk // 2), blk // 2)
+                        w[rows, ds(base, grp)] = got[:, side * grp : (side + 1) * grp]
+
+    cx_o[:, ds(x * hw, hw)] = cown[...]
+    cx_o[:, ds((1 - x) * hw, hw)] = coth[...]
+    mid = fr[...].astype(F32) + dot(cx_o[...], w[...]) + ob[...]
     mid_o[...] = mid
     r = lax.rsqrt(jnp.mean(mid * mid, axis=1, keepdims=True) + EPS)
-    cs[...] = (mid * r * gain[...]).astype(BF)
+    tmp[...] = (mid * r * gain[...]).astype(BF)
     for p in range(nz * ny):
-        a_o[:, p * blk : (p + 1) * blk] = cs[:, ds(place(sc, p, nz, ny) * blk, blk)]
+        a_o[:, p * blk : (p + 1) * blk] = tmp[:, ds(place(sc, p, nz, ny) * blk, blk)]
 
 
 def mlp_kernel(
@@ -244,27 +257,32 @@
 
 
 def mid_kernel(
-    sc, da, dr, bo, br, mid, do, gain, db, cr, wa0, wa1, wb,
+    sc, da0, da1, dr0, dr1, bo0, bo1, br0, br1, mid, do, gain, db, cx, w,
     blk_o, dmid_o, dco_o, dcs_o, wo_o, ws_o, vec_o,
-    tmp, dat, dcx, acc_o, acc_s, *, nz, ny, nx, blk, wc,
+    tmp, dcx, acc, *, nz, ny, nx, blk, grp,
 ):
     i = pl.program_id(0)
-    x, c = sc[3], sc[2]
-    hw = bo.shape[1] // nx
+    x = sc[3]
+    hw = tmp.shape[1] // nx
 
     @pl.when(i == 0)
     def _():
         vec_o[...] = jnp.zeros_like(vec_o)
-        acc_o[...] = jnp.zeros_like(acc_o)
-        acc_s[...] = jnp.zeros_like(acc_s)
+        acc[...] = jnp.zeros_like(acc)
+
+    def total(parts, lo, hi):
+        got = parts[0][:, lo:hi].astype(F32)
+        for part in parts[1:]:
+            got = got + part[:, lo:hi].astype(F32)
+        return got
 
     mv = mid[...]
     for xrel in range(nx):
-        part = bo[:, xrel * hw : (xrel + 1) * hw] + br[:, xrel * hw : (xrel + 1) * hw].astype(F32)
+        part = total((bo0, bo1, br0, br1), xrel * hw, (xrel + 1) * hw)
         tmp[:, ds(lax.rem(x + xrel, nx) * hw, hw)] = part
     blk_o[...] = (mv + tmp[...] + db[...]).astype(BF)
     for p in range(nz * ny):
-        part = da[:, p * blk : (p + 1) * blk] + dr[:, p * blk : (p + 1) * blk].astype(F32)
+        part = total((da0, da1, dr0, dr1), p * blk, (p + 1) * blk)
         tmp[:, ds(place(sc, p, nz, ny) * blk, blk)] = part
     dact = tmp[...]
     r = lax.rsqrt(jnp.mean(mv * mv, axis=1, keepdims=True) + EPS)
@@ -274,81 +292,84 @@
     dmid = dout + r * (dn - n * jnp.mean(dn * n, axis=1, keepdims=True))
     dmid_o[...] = dmid
     dattn = dmid.astype(BF)
-    dat[...] = dattn
     vec_o[0:1, :] += jnp.sum(dact * n, axis=0, keepdims=True)
     vec_o[1:2, :] += jnp.sum(dattn.astype(F32), axis=0, keepdims=True)
     vec_o[2:3, :] += jnp.sum(dout, axis=0, keepdims=True)
-    k = nz * blk
-    sums = [None, None]
-    crt = cr[...].T
-    for xrel in range(nx):
-        for crel in range(2):
-            base = lax.rem(x + xrel, nx) * 2 + lax.rem(c + crel, 2)
-            piece = dat[:, ds(base * wc, wc)]
-            for yrel in range(2):
-                got = dot_last(piece, out_weight((wa0, wa1), wb, xrel, crel, yrel))
-                sums[yrel] = got if sums[yrel] is None else sums[yrel] + got
-            acc = acc_o if crel == 0 else acc_s
-            acc[:, xrel * wc : (xrel + 1) * wc] += dot(crt, piece)
-    for p in range(nz * ny):
-        part = sums[p // nz][:, (p % nz) * blk : (p % nz + 1) * blk]
-        dcx[:, ds(place(sc, p, nz, ny) * blk, blk)] = part.astype(BF)
+    dcx[...] = dot_last(dattn, w[...]).astype(BF)
     heads = dco_o.shape[1]
     dco_o[...] = dcx[:, ds(x * heads, heads)]
     dcs_o[...] = dcx[:, ds((1 - x) * heads, heads)]
+    acc[...] += dot(cx[...].T, dattn)
 
     @pl.when(i == pl.num_programs(0) - 1)
     def _():
-        wo_o[...] = acc_o[...].astype(BF)
-        ws_o[...] = acc_s[...].astype(BF)
-
-
-def dact_kernel(
-    sc, dq, dk, dv, own, oth, gain, ar, wa0, wa1, wb0, wb1,
-    da_o, ds_o, wo_o, ws_o, vec_o, tmp, acc, *, nz, ny, blk, grp,
+        for xrel in range(nx):
+            for crel, out in enumerate((wo_o, ws_o)):
+                base = lax.rem(x + xrel, nx) * heads + lax.rem(sc[2] + crel, 2) * grp
+                for p in range(nz * ny):
+                    rows = ds(place(sc, p, nz, ny) * blk, blk)
+                    out[xrel, p] = acc[rows, ds(base, grp)].astype(BF)
+
+
+def gain_part(w, got, cols, hd, grp):
+    total = None
+    for k in range(3):
+        prod = w[:, ds(k * hd + cols, grp)].astype(F32) * got[:, k * grp : (k + 1) * grp]
+        for lo in range(0, grp, 128):
+            part = prod[:, lo : lo + 128]
+            total = part if total is None else total + part
+    return jnp.sum(total.T, axis=0, keepdims=True)
+
+
+def give_kernel(sc, ar, dq, dk, dv, w, o, g_o, *, hd, grp):
+    cat = jnp.concatenate([dq[...], dk[...], dv[...]], axis=1)
+    got = dot(ar[...].T, cat)
+    o[...] = got.astype(BF).reshape(o.shape)
+    g_o[...] = gain_part(w, got, (1 - sc[2]) * grp, hd, grp).reshape(g_o.shape)
+
+
+def keep_kernel(
+    sc, ar, dq, dk, dv, w, rec, gg, gain, qs, vs, vm, gu0, gu1, o, *, nz, ny, nx, hd, grp, blk
 ):
+    p = pl.program_id(0)
+    zy = place(sc, p, nz, ny)
+    cat = jnp.concatenate([dq[...], dk[...], dv[...]], axis=1)
+    got = dot(ar[...].T, cat)
+    o[0, :blk, :] = (got + rec[0].astype(F32)).astype(BF)
+    gsum = (gain_part(w, got, sc[2] * grp, hd, grp) + gg[0]) / gain[:, ds(zy * blk, blk)]
+    nbx = nz * ny // nx
+    here = zy // nbx == sc[3]
+    local = ds(lax.rem(zy, nbx) * blk, blk)
+    lanes = ds(zy * blk, blk)
+    parts = (
+        jnp.where(here, qs[:, local], 0.0),
+        jnp.where(here, vs[:, local], 0.0),
+        vm[1:2, lanes],
+        vm[2:3, lanes],
+        gsum,
+        vm[0:1, lanes],
+    )
+    o[0, blk:, :] = jnp.zeros((o.shape[1] - blk, o.shape[2]), BF)
+    for k, part in enumerate(parts):
+        o[0, blk : blk + 1, k * blk : (k + 1) * blk] = part.astype(BF)
+    ffb = gu0.shape[2]
+    piece = jnp.where(lax.rem(p, 2) == 0, gu0[0], gu1[0])
+    o[0, blk + 1 : blk + 2, ds(sc[2] * ffb, ffb)] = piece.astype(BF)
+
+
+def dact_kernel(sc, dq, dk, dv, w, da_o, ds_o):
     i = pl.program_id(0)
     half = pl.num_programs(0) // 2
-
-    @pl.when(i == 0)
-    def _():
-        vec_o[...] = jnp.zeros_like(vec_o)
-        acc[...] = jnp.zeros_like(acc)
-
-    mine = i >= half
-    f = jnp.where(mine, own[...].astype(F32), oth[...].astype(F32))
-    r = lax.rsqrt(jnp.mean(f * f, axis=1, keepdims=True) + EPS)
-    k = nz * blk
-    sums = [None, None]
-    art = ar[...].T
-    for g, pair in enumerate(((wa0, wa1), (wb0, wb1))):
-        lo, hi = g * grp, (g + 1) * grp
-        cat = jnp.concatenate([dq[:, lo:hi], dk[:, lo:hi], dv[:, lo:hi]], axis=1)
-        for yrel in range(2):
-            got = dot_last(cat, pair[yrel][...].reshape(k, 3 * grp))
-            sums[yrel] = got if sums[yrel] is None else sums[yrel] + got
-        acc[:, g * 3 * grp : (g + 1) * 3 * grp] += dot(art, cat)
-    for p in range(nz * ny):
-        part = sums[p // nz][:, (p % nz) * blk : (p % nz + 1) * blk]
-        tmp[:, ds(place(sc, p, nz, ny) * blk, blk)] = part
-    dact = tmp[...]
-    vec_o[0:1, :] += jnp.sum(dact * (f * r), axis=0, keepdims=True)
-    w = 2 * grp
-    vec_o[1:2, :w] += jnp.sum(dq[...].astype(F32), axis=0, keepdims=True)
-    vec_o[2:3, :w] += jnp.sum(dv[...].astype(F32), axis=0, keepdims=True)
-
-    @pl.when(mine)
+    cat = jnp.concatenate([dq[...], dk[...], dv[...]], axis=1)
+    dact = dot_last(cat, w[...])
+
+    @pl.when(i >= half)
     def _():
         da_o[...] = dact
 
     @pl.when(i < half)
     def _():
         ds_o[...] = dact.astype(BF)
-
-    @pl.when(i == pl.num_programs(0) - 1)
-    def _():
-        wo_o[...] = acc[:, : 3 * grp].astype(BF)
-        ws_o[...] = acc[:, 3 * grp :].astype(BF)
 
 
 def last_kernel(sc, da, dr, dmid, fr, gain, o):
@@ -387,7 +408,6 @@
     ffb = down_proj.shape[0]
     ffx = up_proj.shape[1] // 2
     nj = ffx // ffb
-    wc = grp
     hw = d // nx
 
     def send_w(a, dz=0, dy=0, dc=0):
@@ -407,20 +427,6 @@
                 perm.append((i * nx + j, (i ^ 1) * nx + (j + 1) % nx))
         return lax.ppermute(a, ("wide", "narrow"), perm)
 
-    send = {
-        "z": lambda a, k: send_w(a, dz=k),
-        "y": lambda a, k: send_w(a, dy=k),
-        "x": lambda a, k: send_x(a, k),
-    }
-    size = {"z": nz, "y": ny, "x": nx}
-
-    def gather(a, order):
-        for at, dim in enumerate(order):
-            parts = [a] + [send[dim](a, k) for k in range(1, size[dim])]
-            if at == len(order) - 1:
-                return parts
-            a = jnp.stack(parts)
-
     def pick(flag, a, b):
         return jnp.where(flag == 0, a, b)
 
@@ -429,43 +435,85 @@
             flag, jnp.concatenate([own, oth], axis=axis), jnp.concatenate([oth, own], axis=axis)
         )
 
+    def tie(values, *deps):
+        flat = lax.optimization_barrier((tuple(values), deps))
+        return flat[0]
+
     vectors = (query_bias, value_bias, out_bias, up_bias, down_bias, attn_gain, mlp_gain)
     widths = [piece.shape[0] for piece in vectors]
-    packed = jnp.concatenate(vectors)
-    nv = packed.shape[0]
+    nv = sum(widths)
+    packed = jnp.zeros((nv,), BF)
+    offset = 0
+    for piece, width in zip(vectors, widths):
+        packed = packed + jnp.pad(piece, (offset, nv - offset - width))
+        offset = offset + width
     segs = segment_ids[0]
-    vec_x = send_x(jnp.concatenate([packed, segs.astype(BF)]))
+    tail = jnp.pad(packed, (0, m)) + jnp.pad(segs.astype(BF), (nv, 0))
+    vec_x = send_x(tail)
     vec_xc = send_xc(packed)
-
-    def halves(a):
+    vec_c = send_w(packed, dc=1)
+
+    def halves_of(a):
         return a[:, :grp], a[:, grp:]
 
+    def trade(sides):
+        keep, give = pick(c, sides[0], sides[1]), pick(c, sides[1], sides[0])
+        return in_order(c, keep, send_w(give, dc=1))
+
+    qs, ks, vs, os = [halves_of(a) for a in (query_proj, key_proj, value_proj, out_proj)]
+    pair = trade([jnp.concatenate([qs[e], ks[e], vs[e]], axis=1) for e in range(2)])
     up4 = up_proj.reshape(wr, nj, 2, ffb)
-    qs, ks, vs, os = halves(query_proj), halves(key_proj), halves(value_proj), halves(out_proj)
-    us = (up4[:, :, 0].reshape(wr, ffx), up4[:, :, 1].reshape(wr, ffx))
-    sides = [jnp.concatenate([us[s], os[s], qs[s], ks[s], vs[s]], axis=1) for s in range(2)]
-    keep = pick(c, sides[0], sides[1])
-    give = pick(c, sides[1], sides[0])
-    got = send_w(give, dc=1)
-    vec_c = send_w(packed, dc=1)
-    pair = in_order(c, keep, got)
-    uo = pair[:, : ffx + grp]
+    uo_pair = trade(
+        [jnp.concatenate([up4[:, :, e].reshape(wr, ffx), os[e]], axis=1) for e in range(2)]
+    )
+
+    def along_z(a):
+        return [a] + [send_w(a, dz=k) for k in range(1, nz)]
+
+    in_z = along_z(pair)
     own_vec = in_order(x, packed[None], vec_x[None, :nv])
     oth_vec = in_order(x, vec_c[None], vec_xc[None])
     vec4 = in_order(c, own_vec, oth_vec).reshape(-1)
     tail_rows = 16
-    vec_block = jnp.pad(vec4, (0, tail_rows * 3 * grp - vec4.shape[0])).reshape(tail_rows, 3 * grp)
-    qkv_block = jnp.concatenate([pair[:, ffx + grp :], vec_block], axis=0)
-
-    wa = gather(qkv_block, "zy")
-    frames_oth = send_x(frames)
-    wb = [send_w(a[:, : 2 * wr], dc=1) for a in wa]
-    dout_par = send_w(out_grad, dc=1)
-    uo_all = gather(uo, "xzy")
-    down_all = gather(down_proj, "zyx")
-    wo_par = send_w(jnp.stack([a[:, :, :, ffx:] for a in uo_all]), dc=1)
-
-    count = nw * nx * nv // nb
+    count = vec4.shape[0]
+    vec_block = jnp.pad(vec4, (0, tail_rows * 3 * grp - count)).reshape(tail_rows, 3 * grp)
+    vec_z = along_z(vec_block)
+    in_y = jnp.stack([jnp.concatenate([a, b]) for a, b in zip(in_z, vec_z)])
+    wa = [in_y, send_w(in_y, dy=1)]
+    wb = [send_w(a, dc=1) for a in wa]
+
+    (frames_go,) = tie((frames,), vec_x, vec_xc)
+    frames_oth = send_x(frames_go)
+    (dout_go,) = tie((out_grad,), vec_xc)
+    dout_par = send_w(dout_go, dc=1)
+    (uo_go,) = tie((uo_pair,), frames_oth)
+    uo_x = jnp.stack([uo_pair, send_x(uo_go)])
+
+    out_pair = uo_pair[:, ffx:]
+    out_block = jnp.concatenate([out_pair[:blk // 2], out_pair[blk // 2 :]], axis=1)
+    (dn,) = tie((jnp.concatenate([down_proj, out_block]),), *in_z[1:])
+    dn_z = along_z(dn)
+    dn_y = jnp.stack(dn_z)
+    (dn_go,) = tie((dn_y,), wa[1])
+    dn_y = [dn_y, send_w(dn_go, dy=1)]
+    ow = jnp.stack([a[:, ffb:] for a in dn_y])
+    out_w = [ow, send_x(ow)]
+    out_wc = [send_w(a, dc=1) for a in out_w]
+    hz = nz // 2
+    dns = [jnp.stack([a[e::2, :ffb] for a in dn_y]) for e in range(2)]
+
+    ups = [uo_x[:, :, e * (ffx // 2) : (e + 1) * (ffx // 2)] for e in range(2)]
+    ups = [pick(z % 2, ups[0], ups[1]), pick(z % 2, ups[1], ups[0])]
+
+    def up_part(e, *deps):
+        use = tie((ups[e], ups[1 - e]), *deps)
+        got = [use[0]] + [send_w(use[k % 2], dz=k) for k in range(1, nz)]
+        return jnp.stack(got), got[-1]
+
+    up_z0, z0_done = up_part(0, *dn_z[1:])
+    up_z1, _ = up_part(1, z0_done)
+    up_y = [[a, send_w(a, dy=1)] for a in (up_z0, up_z1)]
+
     table = jnp.stack([a[:, 2 * wr :].reshape(nz, -1)[:, :count] for a in wa]).reshape(nb, count)
     here = jnp.arange(nb)
     back = lax.rem(y + ny - here % ny, ny) * nz + lax.rem(z + nz - here // ny, nz)
@@ -476,12 +524,8 @@
         full_vec.append(table[:, offset : offset + width].reshape(1, -1))
         offset = offset + width
     b_query, b_value, b_out, b_up, b_down, g_attn, g_mlp = full_vec
-
-    def own_heads(v):
-        mine = lax.dynamic_slice(v, (0, x * 2 * grp), (1, 2 * grp))
-        return pick(c, mine, jnp.concatenate([mine[:, grp:], mine[:, :grp]], axis=1))
-
-    qb, vb = own_heads(b_query), own_heads(b_value)
+    qb = lax.dynamic_slice(b_query, (0, x * 2 * grp), (1, 2 * grp))
+    vb = lax.dynamic_slice(b_value, (0, x * 2 * grp), (1, 2 * grp))
     ub = lax.dynamic_index_in_dim(b_up.reshape(nb, 2, ffb), c, axis=1)
 
     sc_at = jnp.arange(5, dtype=jnp.int32)
@@ -494,148 +538,163 @@
     rb = min(256, m)
     steps = rows // rb
     per = m // rb
-    wspec = whole((nz, 2 * wr, 3 * grp))
+    hd = 2 * grp
+    wspec = whole((d, 3 * hd))
+    wpart = whole((nz, 2 * wr, 3 * grp))
     dims = dict(nz=nz, ny=ny, blk=blk)
     row_own = pl.BlockSpec((rb, d), lambda i, sc: (i % per, 0))
     wide_row = pl.BlockSpec((rb, d), lambda i, sc: (i, 0))
-    heads_row = pl.BlockSpec((rb, 2 * grp), lambda i, sc: (i, 0))
-    q, k, v, act_one = call(
+    heads_row = pl.BlockSpec((rb, hd), lambda i, sc: (i, 0))
+    q, k, v, act_one, w_in = call(
         functools.partial(qkv_kernel, grp=grp, **dims),
         sc,
-        (frames, frames_oth, g_attn, qb, vb, wa[0], wa[1], wb[0], wb[1]),
+        (frames, frames_oth, g_attn, qb, vb, *wa, *wb),
         (steps,),
-        [row_own, row_own, whole((1, d)), whole((1, 2 * grp)), whole((1, 2 * grp))] + [wspec] * 4,
-        [heads_row, heads_row, heads_row, wide_row],
-        [sds((rows, 2 * grp), BF)] * 3 + [sds((rows, d), BF)],
+        [row_own, row_own, whole((1, d)), whole((1, hd)), whole((1, hd))] + [wpart] * 4,
+        [heads_row, heads_row, heads_row, wide_row, wspec],
+        [sds((rows, hd), BF)] * 3 + [sds((rows, d), BF), sds((d, 3 * hd), BF)],
         [pltpu.VMEM((rb, d), BF)],
     )
 
-    pairs = 2 * grp // 128
+    pairs = hd // 128
     qblk = min(256, rows)
-    rel_pair = pl.BlockSpec((rows, 128), lambda i, sc: (0, i))
-
-    def abs_map(i, sc):
-        return (0, lax.rem(i + sc[2] * (pairs // 2), pairs))
-
-    abs_pair = pl.BlockSpec((rows, 128), abs_map)
+    pair_spec = pl.BlockSpec((rows, 128), lambda i, sc: (0, i))
     ctx, lse = call(
         functools.partial(attn_kernel, qb=qblk),
         sc,
         (segc, segr, q, k, v),
         (pairs,),
-        [whole((rows, 1)), whole((1, rows)), rel_pair, rel_pair, rel_pair],
-        [abs_pair, whole((rows, 128))],
-        [sds((rows, 2 * grp), BF), sds((rows, 128), F32)],
+        [whole((rows, 1)), whole((1, rows)), pair_spec, pair_spec, pair_spec],
+        [pair_spec, whole((rows, 128))],
+        [sds((rows, hd), BF), sds((rows, 128), F32)],
         [pltpu.VMEM((rows, rows), F32)],
     )
-
-    def split_rows(a):
-        return (
-            lax.dynamic_slice(a, (x * m, 0), (m, a.shape[1])),
-            lax.dynamic_slice(a, ((1 - x) * m, 0), (m, a.shape[1])),
+    (ctx,) = tie((ctx,), z0_done)
+    ctx_own = lax.dynamic_slice(ctx, (x * m, 0), (m, hd))
+    ctx_oth = send_x(lax.dynamic_slice(ctx, ((1 - x) * m, 0), (m, hd)))
+
+    ospec = whole((d, d))
+    fsteps = m // rb
+    owpart = whole((ny, nz, blk // 2, hd))
+    ctx_full, mid, act_own, w_out = call(
+        functools.partial(out_kernel, nx=nx, grp=grp, **dims),
+        sc,
+        (ctx_own, ctx_oth, frames, b_out, g_mlp, out_w[0], out_wc[0], out_w[1], out_wc[1]),
+        (fsteps,),
+        [heads_row, heads_row, wide_row, whole((1, d)), whole((1, d))] + [owpart] * 4,
+        [wide_row, wide_row, wide_row, ospec],
+        [sds((m, d), BF), sds((m, d), F32), sds((m, d), BF), sds((d, d), BF)],
+        [pltpu.VMEM((rb, d), BF)],
+    )
+    act_par = send_w(act_own, dc=1)
+    dn0_x = send_x(dns[0])
+    (dn1_go,) = tie((dns[1],), ctx_oth, dn0_x)
+    dn_x = [[dns[0], dn0_x], [dns[1], send_x(dn1_go)]]
+
+    kk = nz * blk
+
+    def feed_forward(odd):
+        def at(t, sc):
+            zy = place(sc, (t // hz) * nz + odd + 2 * (t % hz), nz, ny)
+            return zy, lax.rem(sc[3] + nx - zy // nj, nx), lax.rem(zy, nj)
+
+        def up_in(t, sc):
+            _, xrel, j = at(t, sc)
+            return (0, xrel, 0, j % ny)
+
+        def up_out(t, sc):
+            _, xrel, j = at(t, sc)
+            return (xrel, 0, j % ny)
+
+        upspec = pl.BlockSpec((nz, 1, blk, ffb), up_in)
+        dnspec = pl.BlockSpec((1, 1, ffb, hw), lambda t, sc: (t // hz, t % hz, 0, 0))
+        bspec = pl.BlockSpec((1, 1, ffb), lambda t, sc: (at(t, sc)[0], 0, 0))
+        tspec = pl.BlockSpec((1, 1, ffb), lambda t, sc: (t, 0, 0))
+        return call(
+            mlp_kernel,
+            sc,
+            (act_own, act_par, out_grad, dout_par, ub, *up_y[odd], *dn_x[odd]),
+            (ny * hz,),
+            [whole((m, d))] * 4 + [bspec, upspec, upspec, dnspec, dnspec],
+            [whole((m, d))] * 4
+            + [pl.BlockSpec((1, kk, ffb), up_out)] * 2
+            + [pl.BlockSpec((1, ffb, hw), lambda t, sc: (t, 0, 0))] * 2
+            + [tspec],
+            [sds((m, d), F32), sds((m, d), BF), sds((m, d), F32), sds((m, d), BF)]
+            + [sds((nx, kk, ny * ffb), BF)] * 2
+            + [sds((ny * hz, ffb, hw), BF)] * 2
+            + [sds((ny * hz, 1, ffb), F32)],
+            [
+                pltpu.VMEM((2 * m, d), BF),
+                pltpu.VMEM((d, 2 * m), BF),
+                pltpu.VMEM((2 * m, d), BF),
+                pltpu.VMEM((2 * m, d), F32),
+                pltpu.VMEM((2 * m, d), F32),
+            ],
         )
 
-    ctx_own, ctx_give = split_rows(ctx)
-    ctx_oth = send_x(ctx_give)
-
-    ospec = pl.BlockSpec(
-        (nz, nx, blk, wc), lambda i, sc: (0, 0, 0, ffx // wc), pipeline_mode=pl.Buffered(1)
-    )
-    obspec = whole((2, nz, nx, blk, wc))
-    fsteps = m // rb
-    half_row = pl.BlockSpec((rb, 2 * grp), lambda i, sc: (i, 0))
-    ctx_rel, mid, act_own = call(
-        functools.partial(out_kernel, nx=nx, wc=wc, **dims),
+    halves = []
+    for odd in range(2):
+        got = feed_forward(odd)
+        if odd:
+            got = tie(got, halves[0]["gd_got"], halves[0]["gu_raw"])
+        bo, bo_give, da, da_give, gu, gu_give, gd, gd_give, g_up = got
+        gu_raw = send_w(gu_give, dy=-1)
+        halves.append(
+            dict(
+                bo=bo,
+                da=da,
+                gu=gu.reshape(nx, nz, blk, ny * ffb),
+                gd=gd,
+                g_up=g_up,
+                bo_got=send_w(bo_give, dc=1),
+                da_got=send_w(da_give, dc=1),
+                gd_got=send_x(gd_give),
+                gu_raw=gu_raw,
+                gu_got=gu_raw.reshape(nx, nz, blk, ny * ffb),
+            )
+        )
+
+    def first_sums(h):
+        gd = add_low(h["gd"], h["gd_got"]).astype(BF)
+        gu = [add_low(h["gu"][:, e], h["gu_got"][:, e]).astype(BF) for e in range(nz)]
+        return gd, gu
+
+    gd_0, gu_0 = first_sums(halves[0])
+
+    mid_args = (
+        halves[0]["da"], halves[1]["da"], halves[0]["da_got"], halves[1]["da_got"],
+        halves[0]["bo"], halves[1]["bo"], halves[0]["bo_got"], halves[1]["bo_got"],
+    )
+    block_out, dmid, dctx_own, dctx_give, wo, wo_give, vec_mid = call(
+        functools.partial(mid_kernel, nx=nx, grp=grp, **dims),
         sc,
-        (ctx_own, ctx_oth, frames, b_out, g_mlp, uo_all[0], uo_all[1], wo_par),
+        (*mid_args, mid, out_grad, g_mlp, b_down, ctx_full, w_out),
         (fsteps,),
-        [half_row, half_row, wide_row, whole((1, d)), whole((1, d)), ospec, ospec, obspec],
-        [wide_row, wide_row, wide_row],
-        [sds((m, d), BF), sds((m, d), F32), sds((m, d), BF)],
-        [pltpu.VMEM((rb, d), BF), pltpu.VMEM((rb, d), F32)],
-    )
-    act_par = send_w(act_own, dc=1)
-
-    def up_map(t, sc):
-        zy = place(sc, t, nz, ny)
-        xrel = lax.rem(sc[3] + nx - zy // nj, nx)
-        return xrel, zy % nj
-
-    def up_in(t, sc):
-        xrel, j = up_map(t, sc)
-        return (0, xrel, 0, j)
-
-    def up_out(t, sc):
-        xrel, j = up_map(t, sc)
-        return (xrel, 0, j)
-
-    upspec = pl.BlockSpec((nz, 1, blk, ffb), up_in)
-    dnspec = pl.BlockSpec((1, 1, ffb, hw), lambda t, sc: (t // nz, t % nz, 0, 0))
-    bspec = pl.BlockSpec((1, 1, ffb), lambda t, sc: (place(sc, t, nz, ny), 0, 0))
-    kk = nz * blk
-    bo, bo_give, da, da_give, gu, gu_give, gd, gd_give, g_up = call(
-        mlp_kernel,
-        sc,
-        (act_own, act_par, out_grad, dout_par, ub, uo_all[0], uo_all[1], down_all[0], down_all[1]),
-        (nb,),
-        [whole((m, d))] * 4 + [bspec, upspec, upspec, dnspec, dnspec],
-        [whole((m, d))] * 4
-        + [pl.BlockSpec((1, kk, ffb), up_out)] * 2
-        + [pl.BlockSpec((1, ffb, hw), lambda t, sc: (t, 0, 0))] * 2
-        + [bspec],
-        [sds((m, d), F32), sds((m, d), BF), sds((m, d), F32), sds((m, d), BF)]
-        + [sds((nx, kk, nj * ffb), BF)] * 2
-        + [sds((nb, ffb, hw), BF)] * 2
-        + [sds((nb, 1, ffb), F32)],
-        [
-            pltpu.VMEM((2 * m, d), BF),
-            pltpu.VMEM((d, 2 * m), BF),
-            pltpu.VMEM((2 * m, d), BF),
-            pltpu.VMEM((2 * m, d), F32),
-            pltpu.VMEM((2 * m, d), F32),
-        ],
-    )
-    da_got = send_w(da_give, dc=1)
-    bo_got = send_w(bo_give, dc=1)
-    gd_got = send_x(gd_give)
-    gu_got = send_w(gu_give, dy=1)
-
-    gblk, dmid, dctx_own, dctx_give, wo, wo_give, vec_mid = call(
-        functools.partial(mid_kernel, nx=nx, wc=wc, **dims),
-        sc,
-        (
-            da, da_got, bo, bo_got, mid, out_grad, g_mlp, b_down, ctx_rel,
-            uo_all[0], uo_all[1], wo_par,
-        ),
-        (fsteps,),
-        [wide_row] * 6 + [whole((1, d)), whole((1, d)), wide_row, ospec, ospec, obspec],
-        [wide_row, wide_row, half_row, half_row, whole((d, nx * wc)), whole((d, nx * wc))]
+        [wide_row] * 10 + [whole((1, d)), whole((1, d)), wide_row, ospec],
+        [wide_row, wide_row, heads_row, heads_row]
+        + [whole((nx, nb, blk, grp))] * 2
         + [whole((8, d))],
-        [sds((m, d), BF), sds((m, d), F32), sds((m, 2 * grp), BF), sds((m, 2 * grp), BF)]
-        + [sds((d, nx * wc), BF)] * 2
+        [sds((m, d), BF), sds((m, d), F32), sds((m, hd), BF), sds((m, hd), BF)]
+        + [sds((nx, nb, blk, grp), BF)] * 2
         + [sds((8, d), F32)],
-        [
-            pltpu.VMEM((rb, d), F32),
-            pltpu.VMEM((rb, d), BF),
-            pltpu.VMEM((rb, d), BF),
-            pltpu.VMEM((d, nx * wc), F32),
-            pltpu.VMEM((d, nx * wc), F32),
-        ],
-    )
-    block_out = gblk
-    dctx_oth = send_x(dctx_give)
-    wo_got = send_w(wo_give, dc=1)
-    dctx = in_order(x, dctx_own, dctx_oth)
-
-    dq, dk, dv = call(
+        [pltpu.VMEM((rb, d), F32), pltpu.VMEM((rb, d), BF), pltpu.VMEM((d, d), F32)],
+    )
+    dctx = in_order(x, dctx_own, send_x(dctx_give))
+    wo = add_low(wo, send_w(wo_give, dc=1)).astype(BF)
+    wo_got = send_x(wo[1])
+
+    gd_1, gu_1 = first_sums(halves[1])
+    (dctx,) = tie((dctx,), gd_1, gu_1)
+    dq, dk, dv, qsum, vsum = call(
         functools.partial(attn_back_kernel, qb=qblk),
         sc,
         (segc, segr, q, k, v, dctx, lse),
         (pairs,),
-        [whole((rows, 1)), whole((1, rows)), rel_pair, rel_pair, rel_pair, abs_pair]
+        [whole((rows, 1)), whole((1, rows)), pair_spec, pair_spec, pair_spec, pair_spec]
         + [whole((rows, 128))],
-        [rel_pair] * 3,
-        [sds((rows, 2 * grp), BF)] * 3,
+        [pair_spec] * 3 + [pl.BlockSpec((1, 128), lambda i, sc: (0, i))] * 2,
+        [sds((rows, hd), BF)] * 3 + [sds((1, hd), F32)] * 2,
         [
             pltpu.VMEM((rows, rows), F32),
             pltpu.VMEM((rows, 128), F32),
@@ -643,94 +702,110 @@
         ],
     )
 
-    gd0 = [add_low(gd[e : e + nz], gd_got[e : e + nz]).astype(BF) for e in range(0, nb, nz)]
-    gd1 = add_low(gd0[0], *[send_w(gd0[e], dy=-e) for e in range(1, ny)]).astype(BF)
-    down_grad = add_low(gd1[0], *[send_w(gd1[e], dz=-e) for e in range(1, nz)])
-
-    gu = gu.reshape(nx, nz, blk, ffx)
-    gu_got = gu_got.reshape(nx, nz, blk, ffx)
-    gu0 = [add_low(gu[:, e], gu_got[:, e]).astype(BF) for e in range(nz)]
-    gu1 = add_low(gu0[0], *[send_w(gu0[e], dz=-e) for e in range(1, nz)]).astype(BF)
-    gu2 = add_low(gu1[0], *[send_x(gu1[e], -e) for e in range(1, nx)])
-
-    go0 = add_low(wo, wo_got).astype(BF)
-    go1 = add_low(go0[:, :wc], send_x(go0[:, wc:])).reshape(nb, blk, wc)
+    wo = add_low(wo[0], wo_got).astype(BF)
+    wo = jnp.concatenate([wo[:, : blk // 2], wo[:, blk // 2 :]], axis=2)
+    gd_y = []
+    for yrel in range(ny):
+        parts = [(gd_0, gd_1)[e % 2][yrel * hz + e // 2] for e in range(nz)]
+        gd_y.append(jnp.concatenate([jnp.stack(parts), wo[yrel * nz : (yrel + 1) * nz]], axis=1))
+    gd_2 = add_low(gd_y[0], send_w(gd_y[1], dy=-1)).astype(BF)
+    gu_2 = [in_order(z % 2, a, b, axis=2) for a, b in zip(gu_0, gu_1)]
+    gu_z = [send_w(gu_2[e], dz=-e) for e in range(1, nz)]
+    dq, dk, dv = tie((dq, dk, dv), gd_2)
+
+    def col_rel(e):
+        return pl.BlockSpec((rows, grp), lambda p, sc: (0, lax.rem(sc[2] + e, 2)))
+
+    def block_of(shape):
+        return pl.BlockSpec(shape, lambda p, sc: (p,) + (0,) * (len(shape) - 1))
+
+    ar_spec = pl.BlockSpec((rows, blk), lambda p, sc: (0, p))
+    wrow = pl.BlockSpec((blk, 3 * hd), lambda p, sc: (place(sc, p, nz, ny), 0))
+    wg_give, gain_give = call(
+        functools.partial(give_kernel, hd=hd, grp=grp),
+        sc,
+        (act_one, dq, dk, dv, w_in),
+        (nb,),
+        [ar_spec, col_rel(1), col_rel(1), col_rel(1), wrow],
+        [block_of((1, blk, 3 * grp)), block_of((1, 1, blk))],
+        [sds((nb, blk, 3 * grp), BF), sds((nb, 1, blk), F32)],
+    )
+    wg_got = send_w(wg_give, dc=1)
+    gu_spec = pl.BlockSpec((1, 1, ffb), lambda p, sc: ((p // nz) * hz + (p % nz) // 2, 0, 0))
+    wg = call(
+        functools.partial(keep_kernel, nx=nx, hd=hd, grp=grp, **dims),
+        sc,
+        (
+            act_one, dq, dk, dv, w_in, wg_got, gain_give, g_attn, qsum, vsum, vec_mid,
+            halves[0]["g_up"], halves[1]["g_up"],
+        ),
+        (nb,),
+        [ar_spec, col_rel(0), col_rel(0), col_rel(0), wrow]
+        + [block_of((1, blk, 3 * grp)), block_of((1, 1, blk)), whole((1, d))]
+        + [whole((1, hd)), whole((1, hd)), whole((8, d)), gu_spec, gu_spec],
+        block_of((1, blk + tail_rows, 3 * grp)),
+        sds((nb, blk + tail_rows, 3 * grp), BF),
+    )
+    gq_got = send_w(wg[nz:], dy=-1)
 
     def abs_rows(i, sc):
         return (lax.rem(i + (1 - sc[3]) * per, 2 * per), 0)
 
-    order_row = pl.BlockSpec((rb, 2 * grp), abs_rows)
-    order_wide = pl.BlockSpec((rb, d), abs_rows)
+    order_row = pl.BlockSpec((rb, hd), abs_rows)
     late = pl.BlockSpec((rb, d), lambda i, sc: (jnp.maximum(i - per, 0), 0))
     early = pl.BlockSpec((rb, d), lambda i, sc: (jnp.minimum(i, per - 1), 0))
-    dact, dact_give, wg, wg_give, vec_one = call(
-        functools.partial(dact_kernel, grp=grp, **dims),
+    (dq,) = tie((dq,), wg)
+    dact, dact_give = call(
+        dact_kernel,
         sc,
-        (dq, dk, dv, frames, frames_oth, g_attn, act_one, wa[0], wa[1], wb[0], wb[1]),
+        (dq, dk, dv, w_in),
         (steps,),
-        [order_row] * 3 + [late, early, whole((1, d)), order_wide] + [wspec] * 4,
-        [late, early, whole((d, 3 * grp)), whole((d, 3 * grp)), whole((8, d))],
-        [sds((m, d), F32), sds((m, d), BF)] + [sds((d, 3 * grp), BF)] * 2 + [sds((8, d), F32)],
-        [pltpu.VMEM((rb, d), F32), pltpu.VMEM((d, 6 * grp), F32)],
+        [order_row] * 3 + [wspec],
+        [late, early],
+        [sds((m, d), F32), sds((m, d), BF)],
     )
     dact_got = send_x(dact_give)
-    wg_got = send_w(wg_give, dc=1)
-
-    def other_heads(v):
-        mine = pick(c, v, jnp.concatenate([v[:, grp:], v[:, :grp]], axis=1))
-        return in_order(x, mine, jnp.zeros_like(mine), axis=1)
-
-    core_at = lax.broadcasted_iota(jnp.int32, (nb, 2, ffb), 1)
-    up_bias_grad = jnp.where(core_at == c, g_up.reshape(nb, 1, ffb), 0.0)
-    small = (
-        other_heads(vec_one[1:2, : 2 * grp]),
-        other_heads(vec_one[2:3, : 2 * grp]),
-        vec_mid[1:2],
-        up_bias_grad,
-        vec_mid[2:3],
-        vec_one[0:1],
-        vec_mid[0:1],
-    )
-    vg = jnp.concatenate([g.reshape(nw * nx, width) for g, width in zip(small, widths)], axis=1)
-    vg = vg + send_w(vg, dc=1)
-    vg = vg + send_x(vg)
-    vg = vg + sum(send_w(vg, dy=e) for e in range(1, ny))
-    vg = vg + sum(send_w(vg, dz=e) for e in range(1, nz))
-    flat = lax.dynamic_slice(vg, (w * nx + x, 0), (1, nv)).reshape(-1)
-    vec_out = []
-    offset = 0
-    for width in widths:
-        vec_out.append(flat[offset : offset + width])
-        offset = offset + width
-
-    gq0 = add_low(wg, wg_got).reshape(nb, blk, 3 * grp)
-    gq0 = jnp.concatenate([gq0, go1], axis=2).astype(BF)
-    gq1 = [gq0[e : e + nz] for e in range(0, nb, nz)]
-    gq1 = add_low(gq1[0], *[send_w(gq1[e], dy=-e) for e in range(1, ny)]).astype(BF)
-    gq2 = add_low(gq1[0], *[send_w(gq1[e], dz=-e) for e in range(1, nz)])
-
-    last = jnp.concatenate([gu2, gq2], axis=1)
+
+    gd_3 = add_low(gd_2[0], *[send_w(gd_2[e], dz=-e) for e in range(1, nz)])
+    down_grad = gd_3[:ffb]
+    gu_3 = add_low(gu_2[0], *gu_z).astype(BF)
+    gu_4 = add_low(gu_3[0], send_x(gu_3[1]))
+    go_4 = jnp.concatenate([gd_3[ffb:, :grp], gd_3[ffb:, grp:]], axis=0)
+
+    gq = add_low(wg[:nz], gq_got).astype(BF)
+    (dact_got,) = tie((dact_got,), gq)
+    gq = add_low(gq[0], *[send_w(gq[e], dz=-e) for e in range(1, nz)])
+
+    last = jnp.concatenate([gu_4, gq[:blk], go_4], axis=1)
     mine = lax.dynamic_slice(last, (c * wr, 0), (wr, last.shape[1]))
     theirs = send_w(
         lax.dynamic_slice(last, ((1 - c) * wr, 0), (wr, last.shape[1])).astype(BF), dc=1
     ).astype(F32)
     sides = (pick(c, mine, theirs), pick(c, theirs, mine))
-    up_grad = jnp.concatenate(
-        [s[:, :ffx].reshape(wr, nj, 1, ffb) for s in sides], axis=2
-    ).reshape(wr, 2 * ffx)
+    up_grad = jnp.stack([s[:, :ffx].reshape(wr, nj, ffb) for s in sides], axis=2)
+    up_grad = up_grad.reshape(wr, 2 * ffx)
     weights = []
     for at in range(4):
         lo = ffx + at * grp
         weights.append(jnp.concatenate([s[:, lo : lo + grp] for s in sides], axis=1))
 
-    rowspec = pl.BlockSpec((rb, d), lambda i, sc: (i, 0))
+    small = gq[blk : blk + 2]
+    small = small + send_w(small, dc=1)
+    small = small + send_x(small)
+    who = c * nx + x
+    vec6 = small[0].reshape(6, blk)
+    vec6 = lax.dynamic_slice(vec6, (0, who * (blk // (2 * nx))), (6, blk // (2 * nx)))
+    per_ff = 2 * ffb // (2 * nx)
+    vec_up = lax.dynamic_slice(small[1], (who * per_ff,), (per_ff,))
+    vec_out = (vec6[0], vec6[1], vec6[2], vec_up, vec6[3], vec6[4], vec6[5])
+
     frames_grad = call(
         last_kernel,
         sc,
         (dact, dact_got, dmid, frames, g_attn),
         (fsteps,),
-        [rowspec] * 4 + [whole((1, d))],
-        rowspec,
+        [wide_row] * 4 + [whole((1, d))],
+        wide_row,
         sds((m, d), BF),
     )
     return (block_out, frames_grad, *weights, up_grad, down_grad, *vec_out)
@@ -1108,7 +1183,8 @@
 
 def either(parts, *args):
     d = args[0].shape[1]
-    if parts is None or (d // (parts[0] * parts[1])) % 128 or args[3].shape[1] % 256:
+    blocks = None if parts is None else parts[0] * parts[1]
+    if parts is None or (d // blocks) % 128 or args[3].shape[1] % 256 or parts[0] != 2 * parts[2]:
         return body(*args)
     return fast_body(*parts, *args)
 

time: 551 us -> 495 us (0.90)
  waiting for transfers between devices: 281 us -> 186 us
  Pallas kernels: 137 us -> 160 us
  starting transfers between devices: 63.8 us -> 74 us
  local copies, waits for them, and re-layouts: 30 us -> 36.1 us
    ppermute x41 -> x49, waiting for transfers between devices: 218 us -> 131 us  [send_w(): return lax.ppermute(a, 'wide', perm)]
    pallas_call x8 -> x11, Pallas kernels: 137 us -> 160 us  [call(): pl.pallas_call(kernel, grid_spec=spec, out_shape=out_shape, compiler_para...]
    ppermute x11 -> x14, waiting for transfers between devices: 63.3 us -> 54.9 us  [send_x(): return lax.ppermute(a, 'narrow', [(i, (i + k) % nx) for i in range(nx)])]
    ppermute x11 -> x14, starting transfers between devices: 7.84 us -> 13.7 us  [send_x(): return lax.ppermute(a, 'narrow', [(i, (i + k) % nx) for i in range(nx)])]
    ppermute x41 -> x49, starting transfers between devices: 53.5 us -> 57.7 us  [send_w(): return lax.ppermute(a, 'wide', perm)]
  transfers between devices with their start and end apart: 53 -> 64, of which waited for: 26 -> 25; matrix products, arithmetic and copies ran while one was open for 9% -> 10% of each run, Pallas kernels for 18% -> 26%
where the time goes in v2:
time: 495 us; the launch traced here: 489 us
  waiting for transfers between devices  186 us (38%)
  Pallas kernels  160 us (32%)
  starting transfers between devices  74 us (15%)
  local copies, waits for them, and re-layouts  36.1 us (7%)
  other arithmetic  29.9 us (6%)
    pallas_call x11, Pallas kernels, call(): pl.pallas_call(kernel, grid_spec=spec, out_shape=out_shape, compiler_para...  160 us
    ppermute x49, waiting for transfers between devices, send_w(): return lax.ppermute(a, 'wide', perm)  131 us
    ppermute x49, starting transfers between devices, send_w(): return lax.ppermute(a, 'wide', perm)  57.7 us
    ppermute x14, waiting for transfers between devices, send_x(): return lax.ppermute(a, 'narrow', [(i, (i + k) % nx) for i in range(nx)])  54.9 us
    ppermute x14, starting transfers between devices, send_x(): return lax.ppermute(a, 'narrow', [(i, (i + k) % nx) for i in range(nx)])  13.7 us
  transfers between devices with their start and end apart: 64, of which 25 were waited for; matrix products, arithmetic and copies ran while one was open for 10% of the time, Pallas kernels for 26%

profile of v2, /device:TPU:0, one launch (start us, length us, event | category | flops | bytes accessed | tf_op | source)
XLA Modules:
  0.0 489.4 jit_solution(10332609621679423684)
XLA Ops:
  27.8 10.6 %collective-permute-start.5 = (bf16[128,768]{1,0:T(8,128)(2,1)S(1)}, bf16[128,768]{1,0:T(8,128)(2,1)S(1)}, u32[]{:S(2)}, u32[]{:S(2)}) collective-permute-start(bf16[128,768]{1,0:T(8,128)(2,1)S(1)} %maximum_select_fusion.7), channel_id=1, source_target_pairs={{0,8},{2,10},{4,12},{6,14},{8,16},{10,18},{12,20},{14,22},{16,24},... | collective-permute-start | bytes 589832 | tf_op jit(solution)/shard_map/ppermute | solution.py:418
  49.3 8.3 %collective-permute-done.18 = bf16[320,512]{1,0:T(8,128)(2,1)S(1)} collective-permute-done((bf16[320,512]{1,0:T(8,128)(2,1)S(1)}, bf16[320,512]{1,0:T(8,128)(2,1)S(1)}, u32[]{:S(2)}, u32[]{:S(2)}) %collective-permute-start.18) | collective-permute-done | bytes 327712 | tf_op jit(solution)/shard_map/ppermute | solution.py:418
  57.6 12.7 %collective-permute-done.17 = bf16[320,512]{1,0:T(8,128)(2,1)S(1)} collective-permute-done((bf16[320,512]{1,0:T(8,128)(2,1)S(1)}, bf16[320,512]{1,0:T(8,128)(2,1)S(1)}, u32[]{:S(2)}, u32[]{:S(2)}) %collective-permute-start.17) | collective-permute-done | bytes 327712 | tf_op jit(solution)/shard_map/ppermute | solution.py:418
  82.6 14.1 %collective-permute-done.21 = bf16[4,320,512]{2,1,0:T(8,128)(2,1)} collective-permute-done((bf16[4,320,512]{2,1,0:T(8,128)(2,1)S(1)}, bf16[4,320,512]{2,1,0:T(8,128)(2,1)}, u32[]{:S(2)}, u32[]{:S(2)}) %collective-permute-start.21) | collective-permute-done | bytes 1310752 | tf_op jit(solution)/shard_map/ppermute | solution.py:418
  112.5 10.1 %shard_map.280 = (bf16[1024,512]{1,0:T(8,128)(2,1)}, bf16[1024,512]{1,0:T(8,128)(2,1)}, bf16[1024,512]{1,0:T(8,128)(2,1)}, bf16[1024,1024]{1,0:T(8,128)(2,1)}, bf16[1024,1536]{1,0:T(8,128)(2,1)}) custom-call(s32[5]{0:T(128)} %compare_select_fusion.7.sc, bf16[512,1024]{1,0:T(8,128)(2,1)} %fr.3, bf16[512,1024]{1,0:T(8,128)(2,1)} %copy-done.21, ...), custom_call_target="tpu_custom_call" | custom-call | tf_op jit(solution)/shard_map/pallas_call | solution.py:49
  122.5 20.4 %shard_map.281 = (bf16[1024,512]{1,0:T(8,128)(2,1)}, f32[1024,128]{1,0:T(8,128)}) custom-call(s32[5]{0:T(128)} %compare_select_fusion.7.sc, s32[1024,1]{1,0:T(8,128)} %broadcast_select_fusion.2.segc, s32[1,1024]{1,0:T(1,128)} %broadcast_select_fusion.7.segr, bf16[1024,512]{1,0:T(8,128)(2,1)} %get-tuple-element.87.q, bf16[1024,512]{1,0:T(8,128)(2,1)} %get-tuple-element.88.k, ...), custom_call_target="tpu_custom_call" | custom-call | tf_op jit(solution)/shard_map/pallas_call | solution.py:49
  152.2 7.5 %collective-permute-done.20.coth = bf16[512,512]{1,0:T(8,128)(2,1)S(1)} collective-permute-done((bf16[512,512]{1,0:T(8,128)(2,1)S(1)}, bf16[512,512]{1,0:T(8,128)(2,1)S(1)}, u32[]{:S(2)}, u32[]{:S(2)}) %collective-permute-start.20) | collective-permute-done | bytes 524320 | tf_op jit(solution)/shard_map/ppermute | solution.py:421
  161.1 6.6 %shard_map.282 = (bf16[512,1024]{1,0:T(8,128)(2,1)}, f32[512,1024]{1,0:T(8,128)}, bf16[512,1024]{1,0:T(8,128)(2,1)}, bf16[1024,1024]{1,0:T(8,128)(2,1)}) custom-call(s32[5]{0:T(128)} %compare_select_fusion.7.sc, bf16[512,512]{1,0:T(8,128)(2,1)} %get-tuple-element.185.cown, bf16[512,512]{1,0:T(8,128)(2,1)} %copy-done.25, bf16[512,1024]{1,0:T(8,128)(2,1)} %fr.3, ...), custom_call_target="tpu_custom_call" | custom-call | tf_op jit(solution)/shard_map/pallas_call | solution.py:49
  170.0 7.2 %collective-permute-done.33 = bf16[2,128,512]{2,1,0:T(8,128)(2,1)S(1)} collective-permute-done((bf16[2,128,512]{2,1,0:T(8,128)(2,1)S(1)}, bf16[2,128,512]{2,1,0:T(8,128)(2,1)S(1)}, u32[]{:S(2)}, u32[]{:S(2)}) %collective-permute-start.33) | collective-permute-done | bytes 262176 | tf_op jit(solution)/shard_map/ppermute | solution.py:418
  180.4 7.6 %collective-permute-done.31 = bf16[2,128,512]{2,1,0:T(8,128)(2,1)} collective-permute-done((bf16[2,128,512]{2,1,0:T(8,128)(2,1)S(1)}, bf16[2,128,512]{2,1,0:T(8,128)(2,1)}, u32[]{:S(2)}, u32[]{:S(2)}) %collective-permute-start.31) | collective-permute-done | bytes 262176 | tf_op jit(solution)/shard_map/ppermute | solution.py:418
  196.0 24.9 %shard_map.283 = (f32[512,1024]{1,0:T(8,128)}, bf16[512,1024]{1,0:T(8,128)(2,1)}, f32[512,1024]{1,0:T(8,128)}, bf16[512,1024]{1,0:T(8,128)(2,1)}, bf16[2,512,512...) custom-call(s32[5]{0:T(128)} %compare_select_fusion.7.sc, ...), custom_call_target="tpu_custom_call" | custom-call | tf_op jit(solution)/shard_map/pallas_call | solution.py:49
  222.8 24.5 %shard_map.284 = (f32[512,1024]{1,0:T(8,128)}, bf16[512,1024]{1,0:T(8,128)(2,1)}, f32[512,1024]{1,0:T(8,128)}, bf16[512,1024]{1,0:T(8,128)(2,1)}, bf16[2,512,512...) custom-call(s32[5]{0:T(128)} %compare_select_fusion.7.sc, ...), custom_call_target="tpu_custom_call" | custom-call | tf_op jit(solution)/shard_map/pallas_call | solution.py:49
  252.0 13.8 %shard_map.285 = (bf16[512,1024]{1,0:T(8,128)(2,1)}, f32[512,1024]{1,0:T(8,128)}, bf16[512,512]{1,0:T(8,128)(2,1)}, bf16[512,512]{1,0:T(8,128)(2,1)}, bf16[2,8,1...) custom-call(s32[5]{0:T(128)} %compare_select_fusion.7.sc, ...), custom_call_target="tpu_custom_call" | custom-call | tf_op jit(solution)/shard_map/pallas_call | solution.py:49
  270.9 21.4 %collective-permute-done.43 = bf16[4,256,512]{2,1,0:T(8,128)(2,1)S(1)} collective-permute-done((bf16[4,256,512]{2,1,0:T(8,128)(2,1)}, bf16[4,256,512]{2,1,0:T(8,128)(2,1)S(1)}, u32[]{:S(2)}, u32[]{:S(2)}) %collective-permute-start.43) | collective-permute-done | bytes 1048608 | tf_op jit(solution)/shard_map/ppermute | solution.py:421
  293.5 9.4 %collective-permute-done.46 = bf16[8,128,256]{2,1,0:T(8,128)(2,1)S(1)} collective-permute-done((bf16[8,128,256]{2,1,0:T(8,128)(2,1)S(1)}, bf16[8,128,256]{2,1,0:T(8,128)(2,1)S(1)}, u32[]{:S(2)}, u32[]{:S(2)}) %collective-permute-start.46) | collective-permute-done | bytes 524320 | tf_op jit(solution)/shard_map/ppermute | solution.py:421
  307.2 10.3 %collective-permute-done.42 = bf16[512,512]{1,0:T(8,128)(2,1)S(1)} collective-permute-done((bf16[512,512]{1,0:T(8,128)(2,1)S(1)}, bf16[512,512]{1,0:T(8,128)(2,1)S(1)}, u32[]{:S(2)}, u32[]{:S(2)}) %collective-permute-start.42) | collective-permute-done | bytes 524320 | tf_op jit(solution)/shard_map/ppermute | solution.py:421
  318.9 27.8 %shard_map.286 = (bf16[1024,512]{1,0:T(8,128)(2,1)}, bf16[1024,512]{1,0:T(8,128)(2,1)}, bf16[1024,512]{1,0:T(8,128)(2,1)}, f32[1,512]{1,0:T(1,128)}, f32[1,512]{1,0:T(1,128)}) custom-call(s32[5]{0:T(128)} %compare_select_fusion.7.sc, s32[1024,1]{1,0:T(8,128)} %broadcast_select_fusion.2.segc, s32[1,1024]{1,0:T(1,128)} %broadcast_select_fusion.7.segr, ...), custom_call_target="tpu_custom_call" | custom-call | tf_op jit(solution)/shard_map/pallas_call | solution.py:49
  348.3 9.0 %shard_map.287 = (bf16[8,128,768]{2,1,0:T(8,128)(2,1)}, f32[8,1,128]{2,1,0:T(1,128)}) custom-call(s32[5]{0:T(128)} %compare_select_fusion.7.sc, bf16[1024,1024]{1,0:T(8,128)(2,1)} %get-tuple-element.140.ar, bf16[1024,512]{1,0:T(8,128)(2,1)} %get-tuple-element.151.dq, bf16[1024,512]{1,0:T(8,128)(2,1)} %get-tuple-element.141.dk, ...), custom_call_target="tpu_custom_call" | custom-call | tf_op jit(solution)/shard_map/pallas_call | solution.py:49
  360.8 12.7 %collective-permute-done.51 = bf16[2,128,1024]{2,1,0:T(8,128)(2,1)S(1)} collective-permute-done((bf16[2,128,1024]{2,1,0:T(8,128)(2,1)S(1)}, bf16[2,128,1024]{2,1,0:T(8,128)(2,1)S(1)}, u32[]{:S(2)}, u32[]{:S(2)}) %collective-permute-start.51) | collective-permute-done | bytes 524320 | tf_op jit(solution)/shard_map/ppermute | solution.py:418
  373.5 32.3 %collective-permute-done.52 = bf16[2,128,1024]{2,1,0:T(8,128)(2,1)S(1)} collective-permute-done((bf16[2,128,1024]{2,1,0:T(8,128)(2,1)S(1)}, bf16[2,128,1024]{2,1,0:T(8,128)(2,1)S(1)}, u32[]{:S(2)}, u32[]{:S(2)}) %collective-permute-start.52) | collective-permute-done | bytes 524320 | tf_op jit(solution)/shard_map/ppermute | solution.py:418
  406.2 9.8 %shard_map.288 = bf16[8,144,768]{2,1,0:T(8,128)(2,1)} custom-call(s32[5]{0:T(128)} %compare_select_fusion.7.sc, bf16[1024,1024]{1,0:T(8,128)(2,1)} %get-tuple-element.140.ar, bf16[1024,512]{1,0:T(8,128)(2,1)} %get-tuple-element.151.dq, bf16[1024,512]{1,0:T(8,128)(2,1)} %get-tuple-element.141.dk, bf16[1024,512]{1,0:T(8,128)(2,1)} %get-tuple-element.142.dv, ...), custom_call_target="tpu_custom_call" | custom-call | tf_op jit(solution)/shard_map/pallas_call | solution.py:49
  426.3 8.6 %shard_map.289 = (f32[512,1024]{1,0:T(8,128)}, bf16[512,1024]{1,0:T(8,128)(2,1)}) custom-call(s32[5]{0:T(128)} %compare_select_fusion.7.sc, bf16[1024,512]{1,0:T(8,128)(2,1)} %get-tuple-element.151.dq, bf16[1024,512]{1,0:T(8,128)(2,1)} %get-tuple-element.141.dk, bf16[1024,512]{1,0:T(8,128)(2,1)} %get-tuple-element.142.dv, ...), custom_call_target="tpu_custom_call" | custom-call | tf_op jit(solution)/shard_map/pallas_call | solution.py:49
  441.8 10.8 %collective-permute-done.59 = bf16[320,512]{1,0:T(8,128)(2,1)} collective-permute-done((bf16[320,512]{1,0:T(8,128)(2,1)}, bf16[320,512]{1,0:T(8,128)(2,1)}, u32[]{:S(2)}, u32[]{:S(2)}) %collective-permute-start.59) | collective-permute-done | bytes 327712 | tf_op jit(solution)/shard_map/ppermute | solution.py:418
  469.6 7.3 %collective-permute-done.56 = bf16[144,768]{1,0:T(8,128)(2,1)} collective-permute-done((bf16[144,768]{1,0:T(8,128)(2,1)S(1)}, bf16[144,768]{1,0:T(8,128)(2,1)}, u32[]{:S(2)}, u32[]{:S(2)}) %collective-permute-start.56) | collective-permute-done | bytes 221216 | tf_op jit(solution)/shard_map/ppermute | solution.py:418
  (307 shorter events, 159.3 us)
Async XLA Ops:
  26.1 46.1 %collective-permute-start.2 = (bf16[512,1024]{1,0:T(8,128)(2,1)S(1)}, bf16[512,1024]{1,0:T(8,128)(2,1)S(1)}, u32[]{:S(2)}, u32[]{:S(2)}) collective-permute-start(bf16[512,1024]{1,0:T(8,128)(2,1)S(1)} %copy-done.1), channel_id=1, source_target_pairs={{0,1},{1,0},{2,3},{3,2},{4,5},{5,4},{6,7},{7,6},{8,9},{9,8},{10,11... | collective-permute-start | bytes 3145736 | tf_op jit(solution)/shard_map/ppermute | solution.py:421
  42.7 28.9 %collective-permute-start.11 = (bf16[4,144,768]{2,1,0:T(8,128)(2,1)S(1)}, bf16[4,144,768]{2,1,0:T(8,128)(2,1)}, u32[]{:S(2)}, u32[]{:S(2)}) collective-permute-start(bf16[4,144,768]{2,1,0:T(8,128)(2,1)S(1)} %pad_maximum_fusion.6.wa0), channel_id=1, source_target_pairs={{0,4},{2,6},{4,0},{6,2},{8,12},{10,14},{12,8},{14,10},{16,20},{18,... | collective-permute-start | bytes 2654216 | tf_op jit(solution)/shard_map/ppermute | solution.py:418
  57.6 53.9 %collective-permute-start.12 = (bf16[4,144,768]{2,1,0:T(8,128)(2,1)S(1)}, bf16[4,144,768]{2,1,0:T(8,128)(2,1)}, u32[]{:S(2)}, u32[]{:S(2)}) collective-permute-start(bf16[4,144,768]{2,1,0:T(8,128)(2,1)S(1)} %pad_maximum_fusion.6.wa0), channel_id=1, source_target_pairs={{0,2},{2,0},{4,6},{6,4},{8,10},{10,8},{12,14},{14,12},{16,18},{18,... | collective-permute-start | bytes 2654216 | tf_op jit(solution)/shard_map/ppermute | solution.py:418
  77.4 34.1 %collective-permute-start.13 = (bf16[4,144,768]{2,1,0:T(8,128)(2,1)}, bf16[4,144,768]{2,1,0:T(8,128)(2,1)}, u32[]{:S(2)}, u32[]{:S(2)}) collective-permute-start(bf16[4,144,768]{2,1,0:T(8,128)(2,1)} %collective-permute-done.11.wa1), channel_id=1, source_target_pairs={{0,2},{2,0},{4,6},{6,4},{8,10},{10,8},{12,14},{14,12},{16,18},{18,... | collective-permute-start | bytes 2654216 | tf_op jit(solution)/shard_map/ppermute | solution.py:418
  98.5 47.7 %collective-permute-start.23 = (bf16[2,4,64,512]{3,2,1,0:T(8,128)(2,1)}, bf16[2,4,64,512]{3,2,1,0:T(8,128)(2,1)}, u32[]{:S(2)}, u32[]{:S(2)}) collective-permute-start(bf16[2,4,64,512]{3,2,1,0:T(8,128)(2,1)} %pad_maximum_fusion.7.w00), channel_id=1, source_target_pairs={{0,1},{1,0},{2,3},{3,2},{4,5},{5,4},{6,7},{7,6},{8,9},{9,8},{10,11... | collective-permute-start | bytes 1572872 | tf_op jit(solution)/shard_map/ppermute | solution.py:421
  100.2 44.8 %collective-permute-start.27 = (bf16[2,128,512]{2,1,0:T(8,128)(2,1)}, bf16[2,128,512]{2,1,0:T(8,128)(2,1)S(1)}, u32[]{:S(2)}, u32[]{:S(2)}) collective-permute-start(bf16[2,128,512]{2,1,0:T(8,128)(2,1)} %get-tuple-element.100), channel_id=1, source_target_pairs={{0,8},{2,10},{4,12},{6,14},{8,16},{10,18},{12,20},{14,22},{16,24},... | collective-permute-start | bytes 786440 | tf_op jit(solution)/shard_map/ppermute | solution.py:418
  106.2 40.1 %collective-permute-start.28 = (bf16[2,128,512]{2,1,0:T(8,128)(2,1)}, bf16[2,128,512]{2,1,0:T(8,128)(2,1)}, u32[]{:S(2)}, u32[]{:S(2)}) collective-permute-start(bf16[2,128,512]{2,1,0:T(8,128)(2,1)} %get-tuple-element.101), channel_id=1, source_target_pairs={{0,16},{2,18},{4,20},{6,22},{8,24},{10,26},{12,28},{14,30},{16,0},... | collective-permute-start | bytes 786440 | tf_op jit(solution)/shard_map/ppermute | solution.py:418
  111.5 82.6 %collective-permute-start.26 = (bf16[512,1024]{1,0:T(8,128)(2,1)S(1)}, bf16[512,1024]{1,0:T(8,128)(2,1)S(1)}, u32[]{:S(2)}, u32[]{:S(2)}) collective-permute-start(bf16[512,1024]{1,0:T(8,128)(2,1)S(1)} %copy-done), channel_id=1, source_target_pairs={{0,2},{2,0},{4,6},{6,4},{8,10},{10,8},{12,14},{14,12},{16,18},{18,... | collective-permute-start | bytes 3145736 | tf_op jit(solution)/shard_map/ppermute | solution.py:418
  111.5 56.3 %collective-permute-start.32 = (bf16[2,128,512]{2,1,0:T(8,128)(2,1)}, bf16[2,128,512]{2,1,0:T(8,128)(2,1)}, u32[]{:S(2)}, u32[]{:S(2)}) collective-permute-start(bf16[2,128,512]{2,1,0:T(8,128)(2,1)} %get-tuple-element.100), channel_id=1, source_target_pairs={{0,16},{2,18},{4,20},{6,22},{8,24},{10,26},{12,28},{14,30},{16,0},... | collective-permute-start | bytes 786440 | tf_op jit(solution)/shard_map/ppermute | solution.py:418
  159.7 32.8 %collective-permute-start.30 = (bf16[2,2,256,512]{3,2,1,0:T(8,128)(2,1)}, bf16[2,2,256,512]{3,2,1,0:T(8,128)(2,1)}, u32[]{:S(2)}, u32[]{:S(2)}) collective-permute-start(bf16[2,2,256,512]{3,2,1,0:T(8,128)(2,1)} %pad_maximum_fusion.3.dn0), channel_id=1, source_target_pairs={{0,1},{1,0},{2,3},{3,2},{4,5},{5,4},{6,7},{7,6},{8,9},{9,8},{10,11... | collective-permute-start | bytes 3145736 | tf_op jit(solution)/shard_map/ppermute | solution.py:421
  160.2 33.8 %collective-permute-start.29 = (bf16[4,2,128,512]{3,2,1,0:T(8,128)(2,1)}, bf16[4,2,128,512]{3,2,1,0:T(8,128)(2,1)}, u32[]{:S(2)}, u32[]{:S(2)}) collective-permute-start(bf16[4,2,128,512]{3,2,1,0:T(8,128)(2,1)} %pad_maximum_fusion.2.up0), channel_id=1, source_target_pairs={{0,4},{2,6},{4,0},{6,2},{8,12},{10,14},{12,8},{14,10},{16,20},{18,... | collective-permute-start | bytes 3145736 | tf_op jit(solution)/shard_map/ppermute | solution.py:418
  190.3 32.0 %collective-permute-start.34 = (bf16[4,2,128,512]{3,2,1,0:T(8,128)(2,1)}, bf16[4,2,128,512]{3,2,1,0:T(8,128)(2,1)}, u32[]{:S(2)}, u32[]{:S(2)}) collective-permute-start(bf16[4,2,128,512]{3,2,1,0:T(8,128)(2,1)} %pad_maximum_fusion.4.up0), channel_id=1, source_target_pairs={{0,4},{2,6},{4,0},{6,2},{8,12},{10,14},{12,8},{14,10},{16,20},{18,... | collective-permute-start | bytes 3145736 | tf_op jit(solution)/shard_map/ppermute | solution.py:418
  192.5 30.3 %collective-permute-start.35 = (bf16[2,2,256,512]{3,2,1,0:T(8,128)(2,1)}, bf16[2,2,256,512]{3,2,1,0:T(8,128)(2,1)}, u32[]{:S(2)}, u32[]{:S(2)}) collective-permute-start(bf16[2,2,256,512]{3,2,1,0:T(8,128)(2,1)} %pad_maximum_fusion.5.dn0), channel_id=1, source_target_pairs={{0,1},{1,0},{2,3},{3,2},{4,5},{5,4},{6,7},{7,6},{8,9},{9,8},{10,11... | collective-permute-start | bytes 3145736 | tf_op jit(solution)/shard_map/ppermute | solution.py:421
  220.9 26.5 %collective-permute-start.36 = (bf16[4,256,512]{2,1,0:T(8,128)(2,1)}, bf16[4,256,512]{2,1,0:T(8,128)(2,1)S(1)}, u32[]{:S(2)}, u32[]{:S(2)}) collective-permute-start(bf16[4,256,512]{2,1,0:T(8,128)(2,1)} %get-tuple-element.112), channel_id=1, source_target_pairs={{0,1},{1,0},{2,3},{3,2},{4,5},{5,4},{6,7},{7,6},{8,9},{9,8},{10,11... | collective-permute-start | bytes 3145736 | tf_op jit(solution)/shard_map/ppermute | solution.py:421
  222.3 26.3 %collective-permute-start.38 = (bf16[512,1024]{1,0:T(8,128)(2,1)}, bf16[512,1024]{1,0:T(8,128)(2,1)S(1)}, u32[]{:S(2)}, u32[]{:S(2)}) collective-permute-start(bf16[512,1024]{1,0:T(8,128)(2,1)} %get-tuple-element.115), channel_id=1, source_target_pairs={{0,2},{2,0},{4,6},{6,4},{8,10},{10,8},{12,14},{14,12},{16,18},{18,... | collective-permute-start | bytes 3145736 | tf_op jit(solution)/shard_map/ppermute | solution.py:418
  222.3 26.3 %collective-permute-start.40 = (bf16[512,1024]{1,0:T(8,128)(2,1)}, bf16[512,1024]{1,0:T(8,128)(2,1)}, u32[]{:S(2)}, u32[]{:S(2)}) collective-permute-start(bf16[512,1024]{1,0:T(8,128)(2,1)} %get-tuple-element.119), channel_id=1, source_target_pairs={{0,2},{2,0},{4,6},{6,4},{8,10},{10,8},{12,14},{14,12},{16,18},{18,... | collective-permute-start | bytes 3145736 | tf_op jit(solution)/shard_map/ppermute | solution.py:418
  267.4 38.6 %collective-permute-start.44 = (bf16[2,512,512]{2,1,0:T(8,128)(2,1)}, bf16[2,512,512]{2,1,0:T(8,128)(2,1)S(1)}, u32[]{:S(2)}, u32[]{:S(2)}) collective-permute-start(bf16[2,512,512]{2,1,0:T(8,128)(2,1)} %get-tuple-element.130), channel_id=1, source_target_pairs={{0,4},{2,6},{4,0},{6,2},{8,12},{10,14},{12,8},{14,10},{16,20},{18,... | collective-permute-start | bytes 3145736 | tf_op jit(solution)/shard_map/ppermute | solution.py:418
  270.3 32.5 %collective-permute-start.46 = (bf16[8,128,256]{2,1,0:T(8,128)(2,1)S(1)}, bf16[8,128,256]{2,1,0:T(8,128)(2,1)S(1)}, u32[]{:S(2)}, u32[]{:S(2)}) collective-permute-start(bf16[8,128,256]{2,1,0:T(8,128)(2,1)S(1)} %slice_bitcast_fusion), channel_id=1, source_target_pairs={{0,1},{1,0},{2,3},{3,2},{4,5},{5,4},{6,7},{7,6},{8,9},{9,8},{10,11... | collective-permute-start | bytes 1572872 | tf_op jit(solution)/shard_map/ppermute | solution.py:421
  303.2 43.6 %collective-permute-start.47 = (bf16[4,320,512]{2,1,0:T(8,128)(2,1)S(1)}, bf16[4,320,512]{2,1,0:T(8,128)(2,1)S(1)}, u32[]{:S(2)}, u32[]{:S(2)}) collective-permute-start(bf16[4,320,512]{2,1,0:T(8,128)(2,1)S(1)} %fusion), channel_id=1, source_target_pairs={{0,4},{2,6},{4,0},{6,2},{8,12},{10,14},{12,8},{14,10},{16,20},{18,... | collective-permute-start | bytes 3932168 | tf_op jit(solution)/shard_map/ppermute | solution.py:418
  357.3 48.9 %collective-permute-start.48 = (bf16[8,128,768]{2,1,0:T(8,128)(2,1)}, bf16[8,128,768]{2,1,0:T(8,128)(2,1)}, u32[]{:S(2)}, u32[]{:S(2)}) collective-permute-start(bf16[8,128,768]{2,1,0:T(8,128)(2,1)} %get-tuple-element.144), channel_id=1, source_target_pairs={{0,2},{2,0},{4,6},{6,4},{8,10},{10,8},{12,14},{14,12},{16,18},{18,... | collective-permute-start | bytes 4718600 | tf_op jit(solution)/shard_map/ppermute | solution.py:418
  359.9 45.9 %collective-permute-start.52 = (bf16[2,128,1024]{2,1,0:T(8,128)(2,1)S(1)}, bf16[2,128,1024]{2,1,0:T(8,128)(2,1)S(1)}, u32[]{:S(2)}, u32[]{:S(2)}) collective-permute-start(bf16[2,128,1024]{2,1,0:T(8,128)(2,1)S(1)} %maximum_select_fusion.3), channel_id=1, source_target_pairs={{0,16},{2,18},{4,20},{6,22},{8,24},{10,26},{12,28},{14,30},{16,0},... | collective-permute-start | bytes 1572872 | tf_op jit(solution)/shard_map/ppermute | solution.py:418
  359.9 45.9 %collective-permute-start.53 = (bf16[2,128,1024]{2,1,0:T(8,128)(2,1)S(1)}, bf16[2,128,1024]{2,1,0:T(8,128)(2,1)S(1)}, u32[]{:S(2)}, u32[]{:S(2)}) collective-permute-start(bf16[2,128,1024]{2,1,0:T(8,128)(2,1)S(1)} %maximum_select_fusion.4), channel_id=1, source_target_pairs={{0,8},{2,10},{4,12},{6,14},{8,16},{10,18},{12,20},{14,22},{16,24},... | collective-permute-start | bytes 1572872 | tf_op jit(solution)/shard_map/ppermute | solution.py:418
  418.2 36.6 %collective-permute-start.50 = (bf16[4,144,768]{2,1,0:T(8,128)(2,1)}, bf16[4,144,768]{2,1,0:T(8,128)(2,1)}, u32[]{:S(2)}, u32[]{:S(2)}) collective-permute-start(bf16[4,144,768]{2,1,0:T(8,128)(2,1)} %slice.435), channel_id=1, source_target_pairs={{0,4},{2,6},{4,0},{6,2},{8,12},{10,14},{12,8},{14,10},{16,20},{18,... | collective-permute-start | bytes 2654216 | tf_op jit(solution)/shard_map/ppermute | solution.py:418
  423.9 28.7 %collective-permute-start.59 = (bf16[320,512]{1,0:T(8,128)(2,1)}, bf16[320,512]{1,0:T(8,128)(2,1)}, u32[]{:S(2)}, u32[]{:S(2)}) collective-permute-start(bf16[320,512]{1,0:T(8,128)(2,1)} %get-tuple-element.171), channel_id=1, source_target_pairs={{0,16},{2,18},{4,20},{6,22},{8,24},{10,26},{12,28},{14,30},{16,0},... | collective-permute-start | bytes 983048 | tf_op jit(solution)/shard_map/ppermute | solution.py:418
  (73 other events, 902.5 us)
